TPU v7x, 512 devices: a whole 4x8x8 slice. The times are simulated.
512 devices in a mesh: sen: 32 (over y, z_hi), par: 16 (over x, z_lo, core).
Axes of the slice: x: 4, y: 8, z: 8 (z_hi: 4, z_lo: 2; z = z_hi * 2 + z_lo), core: 2. Of those that a mesh axis runs over, the one named last changes fastest.
Arguments:
- vectors: float32 [2, 256, 256], P(None, 'sen'), may hold values from -6 to 6
- observed: float32 [2, 256, 256], P(None, 'sen'), may hold values from -6 to 6
- operator: bfloat16 [2, 128, 256, 6144], P(None, None, 'sen', 'par'), may hold values from -0.15625 to 0.15625
- noise: float32 [256], P('sen'), may hold values from 0.3 to 3
- coefficient: float32 [16, 384], P('par'), may hold values from 0.05 to 0.24
- offsets: int32 [16, 384], P('par'), may hold values from -3 to 3
Outputs:
- residual: float32 [2, 256, 256], P(None, 'sen')
- applied: float32 [2, 256, 256], P(None, 'sen')
All inputs are finite; a program needn't handle non-finite values.
Results may differ from a plain program's by a relative error of at most 0.0018.
Values may be sent and summed in bfloat16 or wider, within the bound.
A program may use at most 64 MiB of HBM per device.

v0:
```python
import math

import jax
import jax.numpy as jnp
from jax import lax
from jax.sharding import PartitionSpec as P

SWEEPS = 4


def padded_2(cells, sides, width):
    for axis, dim in sides:
        count = lax.axis_size(axis)
        ends = count - 1
        head = lax.slice_in_dim(cells, 0, width, axis=dim)
        tail = lax.slice_in_dim(cells, cells.shape[dim] - width, cells.shape[dim], axis=dim)
        cells = jnp.concatenate(
            [
                lax.ppermute(tail, axis, [(i, (i + 1) % count) for i in range(ends)]),
                cells,
                lax.ppermute(head, axis, [((i + 1) % count, i) for i in range(ends)]),
            ],
            axis=dim,
        )
    return cells


def make_basis(length):
    half = length // 2
    times = jnp.arange(length, dtype=jnp.int32)[:, None]
    freqs = jnp.arange(half, dtype=jnp.int32)[None, :]
    phase = (2 * freqs + 1) * times % (2 * length)
    angle = phase.astype(jnp.float32) * (math.pi / length)
    scale = math.sqrt(2.0 / length)
    return jnp.concatenate([jnp.cos(angle), jnp.sin(angle)], axis=1) * scale


def sweep_once(field, padded, coefficient, offsets):
    width = field.shape[-1]
    upper = padded[..., :-2, :]
    lower = padded[..., 2:, :]
    lower_pad = jnp.pad(lower, ((0, 0), (0, 0), (0, 0), (0, 0), (3, 3)))
    linked = jnp.zeros_like(field)
    for shift in range(-3, 4):
        linked = linked + jnp.where(
            offsets == shift, lower_pad[..., 3 + shift : 3 + shift + width], 0.0
        )
    sides = jnp.pad(field, ((0, 0), (0, 0), (0, 0), (0, 0), (1, 1)))
    return field + coefficient * (sides[..., :-2] + sides[..., 2:] + upper + linked - 4.0 * field)


def smooth(field, coefficient, offsets, extend):
    for sweep in range(SWEEPS):
        field = sweep_once(field, extend(field), coefficient, offsets)
    return field


def forward_part(operator, piece):
    count = piece.shape[1]
    rows = piece.shape[2]
    flat = piece.reshape(2, count, rows, piece.shape[3] * piece.shape[4])
    real = jnp.einsum(
        "fsp,frp->frs", operator[0], flat[0], preferred_element_type=jnp.float32
    ) - jnp.einsum("fsp,frp->frs", operator[1], flat[1], preferred_element_type=jnp.float32)
    imag = jnp.einsum(
        "fsp,frp->frs", operator[0], flat[1], preferred_element_type=jnp.float32
    ) + jnp.einsum("fsp,frp->frs", operator[1], flat[0], preferred_element_type=jnp.float32)
    return jnp.stack([real, imag])


def extend_whole(field):
    return padded_2(field, (("par", 3),), 1)


def hessian(record, operator, noise, coefficient, offsets, basis):
    rows, sensors, length = record.shape
    half = length // 2
    grid_rows, width = coefficient.shape
    spectrum = jnp.dot(
        record.reshape(rows * sensors, length), basis, precision=lax.Precision.HIGHEST
    )
    spectrum = spectrum.reshape(rows, sensors, 2, half).transpose(2, 3, 0, 1).astype(jnp.bfloat16)
    real = jnp.einsum(
        "frs,fsp->frp", spectrum[0], operator[0], preferred_element_type=jnp.float32
    ) + jnp.einsum("frs,fsp->frp", spectrum[1], operator[1], preferred_element_type=jnp.float32)
    imag = jnp.einsum(
        "frs,fsp->frp", spectrum[1], operator[0], preferred_element_type=jnp.float32
    ) - jnp.einsum("frs,fsp->frp", spectrum[0], operator[1], preferred_element_type=jnp.float32)
    partial_value = jnp.stack([real, imag]).reshape(2, half, rows, grid_rows, width)
    adjoint = lax.psum(partial_value, "sen")
    smoothed = smooth(adjoint, coefficient, offsets, extend_whole)
    prior = smoothed.astype(jnp.bfloat16)
    forward = forward_part(operator, prior)
    forward = lax.psum(forward, "par")
    forward = forward.transpose(2, 3, 0, 1).reshape(rows * sensors, length)
    back = jnp.dot(forward, basis.T, precision=lax.Precision.HIGHEST).reshape(rows, sensors, length)
    return back + noise[None, :, None] * record


def body(vectors, observed, operator, noise, coefficient, offsets):
    basis = make_basis(vectors.shape[-1])
    residual = observed - hessian(vectors, operator, noise, coefficient, offsets, basis)
    applied = hessian(residual, operator, noise, coefficient, offsets, basis)
    return (residual, applied)


def solution(mesh):
    placed = (
        P(None, "sen", None),
        P(None, "sen", None),
        P(None, None, "sen", "par"),
        P("sen"),
        P("par", None),
        P("par", None),
    )
    return jax.shard_map(
        body,
        mesh=mesh,
        in_specs=placed,
        out_specs=(P(None, "sen", None), P(None, "sen", None)),
        check_vma=False,
    )
```

profile of v0, /device:TPU:1, one launch (start us, length us, event | category | flops | bytes accessed | tf_op | source)
XLA Modules:
  0.0 1003.3 jit_solution(16166331370840971243)
XLA Ops:
  13.1 306.2 %all-reduce.19.cloned.1.call-done = f32[2,128,2,1,384]{4,2,1,0,3:T(2,128)} async-done(((f32[2,128,2,1,384]{4,2,1,0,3:T(2,128)}), f32[2,128,2,1,384]{4,2,1,0,3:T(2,128)}) %all-reduce.19.cloned.1.call-update) | async-done | bytes 786448 | tf_op jit(solution)/shard_map/psum | solution.py:90
  319.3 24.2 %collective-permute-start = (f32[2,128,2,1,384]{4,2,1,0,3:T(2,128)}, f32[2,128,2,1,384]{4,2,1,0,3:T(2,128)S(1)}, u32[]{:S(2)}, u32[]{:S(2)}) collective-permute-start(f32[2,128,2,1,384]{4,2,1,0,3:T(2,128)} %all-reduce.19.cloned.1.call-done), channel_id=1, source_target_pairs={{0,1},{1,2},{2,3},{3,4},{4,5},{5,6},{6,7},{7,8},{8,9},{9,10},{10,1... | collective-permute-start | bytes 2359304 | tf_op jit(solution)/shard_map/ppermute | solution.py:19
  345.5 7.2 collective-permute-done
  352.8 10.5 %collective-permute-done.1 = f32[2,128,2,1,384]{4,2,1,0,3:T(2,128)S(1)} collective-permute-done((f32[2,128,2,1,384]{4,2,1,0,3:T(2,128)}, f32[2,128,2,1,384]{4,2,1,0,3:T(2,128)S(1)}, u32[]{:S(2)}, u32[]{:S(2)}) %collective-permute-start.1) | collective-permute-done | bytes 786464 | tf_op jit(solution)/shard_map/ppermute | solution.py:21
  363.3 8.0 multiply_add_fusion.5
  382.2 9.6 collective-permute-done.3
  391.8 6.8 multiply_add_fusion.4
  409.5 10.5 %collective-permute-done.5 = f32[2,128,2,1,384]{4,2,1,0,3:T(2,128)S(1)} collective-permute-done((f32[2,128,2,1,384]{4,2,1,0,3:T(2,128)S(1)}, f32[2,128,2,1,384]{4,2,1,0,3:T(2,128)S(1)}, u32[]{:S(2)}, u32[]{:S(2)}) %collective-permute-start.5) | collective-permute-done | bytes 786464 | tf_op jit(solution)/shard_map/ppermute | solution.py:21
  419.9 6.8 multiply_add_fusion.3
  437.6 9.7 collective-permute-done.7
  447.3 9.9 add_convert_fusion.1
  459.4 48.9 %psum.29 = f32[2,8,256]{2,1,0:T(8,128)S(1)} all-reduce(f32[2,8,256]{2,1,0:T(8,128)S(1)} %copy_bitcast_fusion.1), channel_id=1, replica_groups=mesh['sen'=32,'par'=16] {'par'}, use_global_device_ids=true, to_apply=%region_1.2 | all-reduce | flops 4096 | bytes 32768 | tf_op jit(solution)/shard_map/psum | solution.py:94
  512.3 297.2 %all-reduce.21.cloned.1.call-done = f32[2,128,2,1,384]{4,2,1,0,3:T(2,128)} async-done(((f32[2,128,2,1,384]{4,2,1,0,3:T(2,128)}), f32[2,128,2,1,384]{4,2,1,0,3:T(2,128)}) %all-reduce.21.cloned.1.call-update) | async-done | bytes 786448 | tf_op jit(solution)/shard_map/psum | solution.py:90
  809.4 24.2 %collective-permute-start.8 = (f32[2,128,2,1,384]{4,2,1,0,3:T(2,128)}, f32[2,128,2,1,384]{4,2,1,0,3:T(2,128)S(1)}, u32[]{:S(2)}, u32[]{:S(2)}) collective-permute-start(f32[2,128,2,1,384]{4,2,1,0,3:T(2,128)} %all-reduce.21.cloned.1.call-done), channel_id=1, source_target_pairs={{0,1},{1,2},{2,3},{3,4},{4,5},{5,6},{6,7},{7,8},{8,9},{9,10},{10,1... | collective-permute-start | bytes 2359304 | tf_op jit(solution)/shard_map/ppermute | solution.py:19
  835.6 7.3 collective-permute-done.8
  842.9 10.5 %collective-permute-done.9 = f32[2,128,2,1,384]{4,2,1,0,3:T(2,128)S(1)} collective-permute-done((f32[2,128,2,1,384]{4,2,1,0,3:T(2,128)}, f32[2,128,2,1,384]{4,2,1,0,3:T(2,128)S(1)}, u32[]{:S(2)}, u32[]{:S(2)}) %collective-permute-start.9) | collective-permute-done | bytes 786464 | tf_op jit(solution)/shard_map/ppermute | solution.py:21
  853.4 8.0 multiply_add_fusion.2
  872.3 9.6 collective-permute-done.11
  881.9 6.8 multiply_add_fusion.1
  899.6 10.5 %collective-permute-done.13 = f32[2,128,2,1,384]{4,2,1,0,3:T(2,128)S(1)} collective-permute-done((f32[2,128,2,1,384]{4,2,1,0,3:T(2,128)S(1)}, f32[2,128,2,1,384]{4,2,1,0,3:T(2,128)S(1)}, u32[]{:S(2)}, u32[]{:S(2)}) %collective-permute-start.13) | collective-permute-done | bytes 786464 | tf_op jit(solution)/shard_map/ppermute | solution.py:21
  910.1 6.8 multiply_add_fusion
  927.7 9.9 collective-permute-done.15
  937.6 6.8 add_convert_fusion
  946.7 48.9 %psum.31 = f32[2,8,256]{2,1,0:T(8,128)S(1)} all-reduce(f32[2,8,256]{2,1,0:T(8,128)S(1)} %copy_bitcast_fusion), channel_id=1, replica_groups=mesh['sen'=32,'par'=16] {'par'}, use_global_device_ids=true, to_apply=%region_3.4 | all-reduce | flops 4096 | bytes 32768 | tf_op jit(solution)/shard_map/psum | solution.py:94
  (76 shorter events, 83.9 us)
Async XLA Ops:
  7.2 312.1 %all-reduce.19.cloned.1.call-start = ((), (), s32[]{:S(2)}) async-start(), calls=%async_computation | async-start | bytes 1572864 | tf_op jit(solution)/shard_map/psum | solution.py:90
  11.8 333.7 %copy-start.5 = (f32[1,384]{1,0:T(1,128)S(1)}, f32[1,384]{1,0:T(1,128)}, u32[]{:S(2)}) copy-start(f32[1,384]{1,0:T(1,128)} %param.10) | copy-start | bytes 4612
  11.8 333.7 %copy-start.6 = (s32[1,384]{1,0:T(1,128)S(1)}, s32[1,384]{1,0:T(1,128)}, u32[]{:S(2)}) copy-start(s32[1,384]{1,0:T(1,128)} %param.11) | copy-start | bytes 4612
  13.1 796.4 %all-reduce.21.cloned.1.call-start = ((), (), s32[]{:S(2)}) async-start(), calls=%async_computation.1 | async-start | bytes 1572864 | tf_op jit(solution)/shard_map/psum | solution.py:90
  319.3 33.5 %collective-permute-start = (f32[2,128,2,1,384]{4,2,1,0,3:T(2,128)}, f32[2,128,2,1,384]{4,2,1,0,3:T(2,128)S(1)}, u32[]{:S(2)}, u32[]{:S(2)}) collective-permute-start(f32[2,128,2,1,384]{4,2,1,0,3:T(2,128)} %all-reduce.19.cloned.1.call-done), channel_id=1, source_target_pairs={{0,1},{1,2},{2,3},{3,4},{4,5},{5,6},{6,7},{7,8},{8,9},{9,10},{10,1... | collective-permute-start | bytes 2359304 | tf_op jit(solution)/shard_map/ppermute | solution.py:19
  343.5 19.8 %collective-permute-start.1 = (f32[2,128,2,1,384]{4,2,1,0,3:T(2,128)}, f32[2,128,2,1,384]{4,2,1,0,3:T(2,128)S(1)}, u32[]{:S(2)}, u32[]{:S(2)}) collective-permute-start(f32[2,128,2,1,384]{4,2,1,0,3:T(2,128)} %all-reduce.19.cloned.1.call-done), channel_id=1, source_target_pairs={{1,0},{2,1},{3,2},{4,3},{5,4},{6,5},{7,6},{8,7},{9,8},{10,9},{11,1... | collective-permute-start | bytes 2359304 | tf_op jit(solution)/shard_map/ppermute | solution.py:21
  371.3 10.8 %collective-permute-start.2 = (f32[2,128,2,1,384]{4,2,1,0,3:T(2,128)S(1)}, f32[2,128,2,1,384]{4,2,1,0,3:T(2,128)S(1)}, u32[]{:S(2)}, u32[]{:S(2)}) collective-permute-start(f32[2,128,2,1,384]{4,2,1,0,3:T(2,128)S(1)} %multiply_add_fusion.5), channel_id=1, source_target_pairs={{0,1},{1,2},{2,3},{3,4},{4,5},{5,6},{6,7},{7,8},{8,9},{9,10},{10,1... | collective-permute-start | bytes 2359304 | tf_op jit(solution)/shard_map/ppermute | solution.py:19
  373.3 18.5 %collective-permute-start.3 = (f32[2,128,2,1,384]{4,2,1,0,3:T(2,128)S(1)}, f32[2,128,2,1,384]{4,2,1,0,3:T(2,128)S(1)}, u32[]{:S(2)}, u32[]{:S(2)}) collective-permute-start(f32[2,128,2,1,384]{4,2,1,0,3:T(2,128)S(1)} %multiply_add_fusion.5), channel_id=1, source_target_pairs={{1,0},{2,1},{3,2},{4,3},{5,4},{6,5},{7,6},{8,7},{9,8},{10,9},{11,1... | collective-permute-start | bytes 2359304 | tf_op jit(solution)/shard_map/ppermute | solution.py:21
  398.6 10.8 %collective-permute-start.4 = (f32[2,128,2,1,384]{4,2,1,0,3:T(2,128)S(1)}, f32[2,128,2,1,384]{4,2,1,0,3:T(2,128)S(1)}, u32[]{:S(2)}, u32[]{:S(2)}) collective-permute-start(f32[2,128,2,1,384]{4,2,1,0,3:T(2,128)S(1)} %multiply_add_fusion.4), channel_id=1, source_target_pairs={{0,1},{1,2},{2,3},{3,4},{4,5},{5,6},{6,7},{7,8},{8,9},{9,10},{10,1... | collective-permute-start | bytes 2359304 | tf_op jit(solution)/shard_map/ppermute | solution.py:19
  400.5 19.4 %collective-permute-start.5 = (f32[2,128,2,1,384]{4,2,1,0,3:T(2,128)S(1)}, f32[2,128,2,1,384]{4,2,1,0,3:T(2,128)S(1)}, u32[]{:S(2)}, u32[]{:S(2)}) collective-permute-start(f32[2,128,2,1,384]{4,2,1,0,3:T(2,128)S(1)} %multiply_add_fusion.4), channel_id=1, source_target_pairs={{1,0},{2,1},{3,2},{4,3},{5,4},{6,5},{7,6},{8,7},{9,8},{10,9},{11,1... | collective-permute-start | bytes 2359304 | tf_op jit(solution)/shard_map/ppermute | solution.py:21
  426.8 10.8 %collective-permute-start.6 = (f32[2,128,2,1,384]{4,2,1,0,3:T(2,128)S(1)}, f32[2,128,2,1,384]{4,2,1,0,3:T(2,128)}, u32[]{:S(2)}, u32[]{:S(2)}) collective-permute-start(f32[2,128,2,1,384]{4,2,1,0,3:T(2,128)S(1)} %multiply_add_fusion.3), channel_id=1, source_target_pairs={{0,1},{1,2},{2,3},{3,4},{4,5},{5,6},{6,7},{7,8},{8,9},{9,10},{10,1... | collective-permute-start | bytes 2359304 | tf_op jit(solution)/shard_map/ppermute | solution.py:19
  428.7 18.6 %collective-permute-start.7 = (f32[2,128,2,1,384]{4,2,1,0,3:T(2,128)S(1)}, f32[2,128,2,1,384]{4,2,1,0,3:T(2,128)}, u32[]{:S(2)}, u32[]{:S(2)}) collective-permute-start(f32[2,128,2,1,384]{4,2,1,0,3:T(2,128)S(1)} %multiply_add_fusion.3), channel_id=1, source_target_pairs={{1,0},{2,1},{3,2},{4,3},{5,4},{6,5},{7,6},{8,7},{9,8},{10,9},{11,1... | collective-permute-start | bytes 2359304 | tf_op jit(solution)/shard_map/ppermute | solution.py:21
  458.8 49.5 %copy-start.2 = (f32[2,8,256]{2,1,0:T(8,128)S(1)}, f32[2,8,256]{2,1,0:T(8,128)}, u32[]{:S(2)}) copy-start(f32[2,8,256]{2,1,0:T(8,128)} %param.6) | copy-start | bytes 49156
  458.8 49.5 %copy-start.3 = (f32[2,8,256]{2,1,0:T(8,128)S(1)}, f32[2,8,256]{2,1,0:T(8,128)}, u32[]{:S(2)}) copy-start(f32[2,8,256]{2,1,0:T(8,128)} %param.7) | copy-start | bytes 49156
  458.9 49.5 %copy-start.4 = (f32[8]{0:T(128)S(1)}, f32[8]{0:T(128)}, u32[]{:S(2)}) copy-start(f32[8]{0:T(128)} %param.9) | copy-start | bytes 100
  508.7 486.9 %copy-start.1 = (f32[2,8,256]{2,1,0:T(8,128)}, f32[2,8,256]{2,1,0:T(8,128)S(1)}, u32[]{:S(2)}) copy-start(f32[2,8,256]{2,1,0:T(8,128)S(1)} %fusion.8) | copy-start | bytes 49156
  809.4 33.5 %collective-permute-start.8 = (f32[2,128,2,1,384]{4,2,1,0,3:T(2,128)}, f32[2,128,2,1,384]{4,2,1,0,3:T(2,128)S(1)}, u32[]{:S(2)}, u32[]{:S(2)}) collective-permute-start(f32[2,128,2,1,384]{4,2,1,0,3:T(2,128)} %all-reduce.21.cloned.1.call-done), channel_id=1, source_target_pairs={{0,1},{1,2},{2,3},{3,4},{4,5},{5,6},{6,7},{7,8},{8,9},{9,10},{10,1... | collective-permute-start | bytes 2359304 | tf_op jit(solution)/shard_map/ppermute | solution.py:19
  833.7 19.8 %collective-permute-start.9 = (f32[2,128,2,1,384]{4,2,1,0,3:T(2,128)}, f32[2,128,2,1,384]{4,2,1,0,3:T(2,128)S(1)}, u32[]{:S(2)}, u32[]{:S(2)}) collective-permute-start(f32[2,128,2,1,384]{4,2,1,0,3:T(2,128)} %all-reduce.21.cloned.1.call-done), channel_id=1, source_target_pairs={{1,0},{2,1},{3,2},{4,3},{5,4},{6,5},{7,6},{8,7},{9,8},{10,9},{11,1... | collective-permute-start | bytes 2359304 | tf_op jit(solution)/shard_map/ppermute | solution.py:21
  861.5 10.8 %collective-permute-start.10 = (f32[2,128,2,1,384]{4,2,1,0,3:T(2,128)S(1)}, f32[2,128,2,1,384]{4,2,1,0,3:T(2,128)S(1)}, u32[]{:S(2)}, u32[]{:S(2)}) collective-permute-start(f32[2,128,2,1,384]{4,2,1,0,3:T(2,128)S(1)} %multiply_add_fusion.2), channel_id=1, source_target_pairs={{0,1},{1,2},{2,3},{3,4},{4,5},{5,6},{6,7},{7,8},{8,9},{9,10},{10,1... | collective-permute-start | bytes 2359304 | tf_op jit(solution)/shard_map/ppermute | solution.py:19
  863.4 18.5 %collective-permute-start.11 = (f32[2,128,2,1,384]{4,2,1,0,3:T(2,128)S(1)}, f32[2,128,2,1,384]{4,2,1,0,3:T(2,128)S(1)}, u32[]{:S(2)}, u32[]{:S(2)}) collective-permute-start(f32[2,128,2,1,384]{4,2,1,0,3:T(2,128)S(1)} %multiply_add_fusion.2), channel_id=1, source_target_pairs={{1,0},{2,1},{3,2},{4,3},{5,4},{6,5},{7,6},{8,7},{9,8},{10,9},{11,1... | collective-permute-start | bytes 2359304 | tf_op jit(solution)/shard_map/ppermute | solution.py:21
  888.8 10.8 %collective-permute-start.12 = (f32[2,128,2,1,384]{4,2,1,0,3:T(2,128)S(1)}, f32[2,128,2,1,384]{4,2,1,0,3:T(2,128)S(1)}, u32[]{:S(2)}, u32[]{:S(2)}) collective-permute-start(f32[2,128,2,1,384]{4,2,1,0,3:T(2,128)S(1)} %multiply_add_fusion.1), channel_id=1, source_target_pairs={{0,1},{1,2},{2,3},{3,4},{4,5},{5,6},{6,7},{7,8},{8,9},{9,10},{10,1... | collective-permute-start | bytes 2359304 | tf_op jit(solution)/shard_map/ppermute | solution.py:19
  890.7 19.4 %collective-permute-start.13 = (f32[2,128,2,1,384]{4,2,1,0,3:T(2,128)S(1)}, f32[2,128,2,1,384]{4,2,1,0,3:T(2,128)S(1)}, u32[]{:S(2)}, u32[]{:S(2)}) collective-permute-start(f32[2,128,2,1,384]{4,2,1,0,3:T(2,128)S(1)} %multiply_add_fusion.1), channel_id=1, source_target_pairs={{1,0},{2,1},{3,2},{4,3},{5,4},{6,5},{7,6},{8,7},{9,8},{10,9},{11,1... | collective-permute-start | bytes 2359304 | tf_op jit(solution)/shard_map/ppermute | solution.py:21
  916.9 10.8 %collective-permute-start.14 = (f32[2,128,2,1,384]{4,2,1,0,3:T(2,128)S(1)}, f32[2,128,2,1,384]{4,2,1,0,3:T(2,128)S(1)}, u32[]{:S(2)}, u32[]{:S(2)}) collective-permute-start(f32[2,128,2,1,384]{4,2,1,0,3:T(2,128)S(1)} %multiply_add_fusion), channel_id=1, source_target_pairs={{0,1},{1,2},{2,3},{3,4},{4,5},{5,6},{6,7},{7,8},{8,9},{9,10},{10,1... | collective-permute-start | bytes 2359304 | tf_op jit(solution)/shard_map/ppermute | solution.py:19
  918.8 18.8 %collective-permute-start.15 = (f32[2,128,2,1,384]{4,2,1,0,3:T(2,128)S(1)}, f32[2,128,2,1,384]{4,2,1,0,3:T(2,128)S(1)}, u32[]{:S(2)}, u32[]{:S(2)}) collective-permute-start(f32[2,128,2,1,384]{4,2,1,0,3:T(2,128)S(1)} %multiply_add_fusion), channel_id=1, source_target_pairs={{1,0},{2,1},{3,2},{4,3},{5,4},{6,5},{7,6},{8,7},{9,8},{10,9},{11,1... | collective-permute-start | bytes 2359304 | tf_op jit(solution)/shard_map/ppermute | solution.py:21
  (1 other events, 3.3 us)
Sparse Core Ops, SparseCore 0:
  13.2 306.0 all-reduce.18
  512.4 296.9 all-reduce.20
where the time goes:
time: 1000 us
  waiting for transfers between devices  736 us (74%)
  blocking collectives  97.8 us (10%)
  starting transfers between devices  79.8 us (8%)
  other arithmetic  63.2 us (6%)
  between operations  14.4 us (1%)
  matrix products  11.1 us (1%)
    psum x2, waiting for transfers between devices, hessian(): adjoint = lax.psum(partial_value, 'sen')  603 us
    psum x2, blocking collectives, hessian(): forward = lax.psum(forward, 'par')  97.8 us
    ppermute x8, waiting for transfers between devices, padded_2(): lax.ppermute(head, axis, [((i + 1) % count, i) for i in range(ends)])  80.9 us
    ppermute x8, starting transfers between devices, padded_2(): lax.ppermute(tail, axis, [(i, (i + 1) % count) for i in range(ends)])  60 us
    ppermute x8, waiting for transfers between devices, padded_2(): lax.ppermute(tail, axis, [(i, (i + 1) % count) for i in range(ends)])  51.8 us
    add x6, other arithmetic, sweep_once(): field + coefficient * (sides[..., :-2] + sides[..., 2:] + upper + linked...  43.3 us
  transfers between devices with their start and end apart: 18, of which 18 were waited for; matrix products, arithmetic and copies ran while one was open for 0% of the time, Pallas kernels for 0%

commit v1 on v0

v1 whole, which is shorter than its diff:
```python
import math

import jax
import jax.numpy as jnp
from jax import lax
from jax.sharding import PartitionSpec as P

SWEEPS = 4


def make_basis(length):
    half = length // 2
    times = jnp.arange(length, dtype=jnp.int32)[:, None]
    freqs = jnp.arange(half, dtype=jnp.int32)[None, :]
    phase = (2 * freqs + 1) * times % (2 * length)
    angle = phase.astype(jnp.float32) * (math.pi / length)
    scale = math.sqrt(2.0 / length)
    return jnp.concatenate([jnp.cos(angle), jnp.sin(angle)], axis=1) * scale


def smooth(field, coefficient, offsets):
    width = field.shape[-1]
    for sweep in range(SWEEPS):
        padded = jnp.pad(field, ((1, 1), (0, 0)))
        upper = padded[:-2]
        lower_pad = jnp.pad(padded[2:], ((0, 0), (3, 3)))
        linked = jnp.zeros_like(field)
        for shift in range(-3, 4):
            linked = linked + jnp.where(
                offsets == shift, lower_pad[:, 3 + shift : 3 + shift + width], 0.0
            )
        sides = jnp.pad(field, ((0, 0), (1, 1)))
        field = field + coefficient * (sides[:, :-2] + sides[:, 2:] + upper + linked - 4.0 * field)
    return field


def hessian(record, operator, noise, coefficient, offsets, basis):
    rows, sensors, length = record.shape
    half = length // 2
    cells = operator.shape[-1]
    spectrum = jnp.dot(
        record.reshape(rows * sensors, length), basis, precision=lax.Precision.HIGHEST
    )
    spectrum = spectrum.reshape(rows, sensors, 2, half).transpose(2, 3, 0, 1).astype(jnp.bfloat16)
    real = jnp.einsum(
        "frs,fsp->frp", spectrum[0], operator[0], preferred_element_type=jnp.float32
    ) + jnp.einsum("frs,fsp->frp", spectrum[1], operator[1], preferred_element_type=jnp.float32)
    imag = jnp.einsum(
        "frs,fsp->frp", spectrum[1], operator[0], preferred_element_type=jnp.float32
    ) - jnp.einsum("frs,fsp->frp", spectrum[0], operator[1], preferred_element_type=jnp.float32)
    planes = jnp.stack([real, imag], axis=1).reshape(half * 2 * rows, cells)
    planes = lax.psum_scatter(planes, "sen", scatter_dimension=0, tiled=True)
    plane = lax.all_to_all(planes, "par", 0, 0, tiled=True)
    prior = smooth(plane, coefficient, offsets).astype(jnp.bfloat16)
    planes = lax.all_to_all(prior, "par", 0, 0, tiled=True)
    planes = lax.all_gather(planes, "sen", axis=0, tiled=True)
    planes = planes.reshape(half, 2, rows, cells)
    flat = (planes[:, 0], planes[:, 1])
    real = jnp.einsum(
        "fsp,frp->frs", operator[0], flat[0], preferred_element_type=jnp.float32
    ) - jnp.einsum("fsp,frp->frs", operator[1], flat[1], preferred_element_type=jnp.float32)
    imag = jnp.einsum(
        "fsp,frp->frs", operator[0], flat[1], preferred_element_type=jnp.float32
    ) + jnp.einsum("fsp,frp->frs", operator[1], flat[0], preferred_element_type=jnp.float32)
    forward = lax.psum(jnp.stack([real, imag]), "par")
    forward = forward.transpose(2, 3, 0, 1).reshape(rows * sensors, length)
    back = jnp.dot(forward, basis.T, precision=lax.Precision.HIGHEST).reshape(rows, sensors, length)
    return back + noise[None, :, None] * record


def body(vectors, observed, operator, noise, coefficient, offsets):
    basis = make_basis(vectors.shape[-1])
    coefficient = lax.all_gather(coefficient, "par", axis=0, tiled=True)
    offsets = lax.all_gather(offsets, "par", axis=0, tiled=True)
    residual = observed - hessian(vectors, operator, noise, coefficient, offsets, basis)
    applied = hessian(residual, operator, noise, coefficient, offsets, basis)
    return (residual, applied)


def solution(mesh):
    placed = (
        P(None, "sen", None),
        P(None, "sen", None),
        P(None, None, "sen", "par"),
        P("sen"),
        P("par", None),
        P("par", None),
    )
    return jax.shard_map(
        body,
        mesh=mesh,
        in_specs=placed,
        out_specs=(P(None, "sen", None), P(None, "sen", None)),
        check_vma=False,
    )
```

time: 1000 us -> 827 us (0.83)
  waiting for transfers between devices: 736 us -> 455 us
  blocking collectives: 97.8 us -> 321 us
  starting transfers between devices: 79.8 us -> 13.3 us
  other arithmetic: 63.2 us -> 3.5 us
    psum x2 -> x0, waiting for transfers between devices: 603 us -> none  [hessian(): adjoint = lax.psum(partial_value, 'sen')]
    reduce_scatter x0 -> x2, waiting for transfers between devices: none -> 449 us  [hessian(): planes = lax.psum_scatter(planes, 'sen', scatter_dimension=0, tiled=True)]
    all_gather x0 -> x4, blocking collectives: none -> 171 us  [the longest x2 135 us: hessian(): planes = lax.all_gather(planes, 'sen', axis=0, tiled=True)]
    ppermute x16 -> x0, waiting for transfers between devices: 133 us -> none  [the longest x8 80.9 us: padded_2(): lax.ppermute(head, axis, [((i + 1) % count, i) for i in range(ends)])]
    ppermute x16 -> x0, starting transfers between devices: 79.8 us -> none  [the longest x8 60 us: padded_2(): lax.ppermute(tail, axis, [(i, (i + 1) % count) for i in range(ends)])]
    add x6, other arithmetic: 43.3 us -> 0.75 us  [smooth(): field + coefficient * (sides[:, :-2] + sides[:, 2:] + upper + linked - 4....]
    psum x2, blocking collectives: 97.8 us -> 126 us  [hessian(): forward = lax.psum(jnp.stack([real, imag]), 'par')]
    all_to_all x0 -> x2, blocking collectives: none -> 24 us  [the longest x1 15.4 us: hessian(): plane = lax.all_to_all(planes, 'par', 0, 0, tiled=True)]
  transfers between devices with their start and end apart: 18 -> 4, of which waited for: 18 -> 3; matrix products, arithmetic and copies ran while one was open for 0% -> 0% of each run, Pallas kernels for 0% -> 0%
where the time goes in v1:
time: 827 us; the launch traced here: 826 us
  waiting for transfers between devices  455 us (55%)
  blocking collectives  321 us (39%)
  between operations  14.4 us (2%)
  starting transfers between devices  13.3 us (2%)
  matrix products  11.1 us (1%)
  local copies, waits for them, and re-layouts  8.35 us (1%)
    reduce_scatter x2, waiting for transfers between devices, hessian(): planes = lax.psum_scatter(planes, 'sen', scatter_dimension=0, tiled=True)  449 us
    all_gather x2, blocking collectives, hessian(): planes = lax.all_gather(planes, 'sen', axis=0, tiled=True)  135 us
    psum x2, blocking collectives, hessian(): forward = lax.psum(jnp.stack([real, imag]), 'par')  126 us
    all_gather x1, blocking collectives, body(): coefficient = lax.all_gather(coefficient, 'par', axis=0, tiled=True)  20 us
  transfers between devices with their start and end apart: 4, of which 3 were waited for; matrix products, arithmetic and copies ran while one was open for 0% of the time, Pallas kernels for 0%

profile of v1, /device:TPU:1, one launch (start us, length us, event | category | flops | bytes accessed | tf_op | source)
XLA Modules:
  0.0 826.2 jit_solution(6979798992075680855)
XLA Ops:
  7.8 0.9 fusion.9
  8.9 1.6 fusion.32
  12.4 1.4 reshape.51
  13.9 229.4 %reduce-scatter.3.cloned.1.call-done = f32[16,384]{1,0:T(8,128)} async-done(((f32[512,384]{1,0:T(8,128)}), f32[16,384]{1,0:T(8,128)}) %reduce-scatter.3.cloned.1.call-update) | async-done | bytes 24592 | tf_op jit(solution)/shard_map/reduce_scatter | solution.py:52
  243.3 1.4 copy.61
  244.7 9.8 %all-to-all-start = ((f32[16,1,384]{2,1,0:T(1,128)}), f32[16,1,384]{2,1,0:T(1,128)S(1)}, u32[]{:S(2)}, u32[]{:S(2)}) async-start(f32[16,1,384]{2,1,0:T(1,128)} %copy.61), calls=%async_computation.1 | async-start | bytes 49152 | tf_op jit(solution)/shard_map/all_to_all | solution.py:53
  254.5 20.0 %all-gather.2 = f32[16,1,384]{2,1,0:T(1,128)S(1)} all-gather(f32[1,1,384]{2,1,0:T(1,128)S(1)} %bitcast.259), channel_id=1, replica_groups=mesh['sen'=32,'par'=16] {'par'}, dimensions={0}, use_global_device_ids=true | all-gather | bytes 26112 | tf_op jit(solution)/shard_map/all_gather | solution.py:73
  274.5 16.3 %all-gather.3 = s32[16,1,384]{2,1,0:T(1,128)S(1)} all-gather(s32[1,1,384]{2,1,0:T(1,128)S(1)} %bitcast.260), channel_id=1, replica_groups=mesh['sen'=32,'par'=16] {'par'}, dimensions={0}, use_global_device_ids=true | all-gather | bytes 26112 | tf_op jit(solution)/shard_map/all_gather | solution.py:74
  291.4 0.6 broadcast.143
  292.0 0.6 reduce
  292.6 0.7 reshape.80
  293.3 3.4 all-to-all-start.1
  297.0 5.6 all-to-all-done.1
  302.7 67.4 %all-gather = bf16[512,1,384]{2,0,1:T(8,128)(2,1)S(1)} all-gather(bf16[16,1,384]{2,0,1:T(8,128)(2,1)S(1)} %copy.70), channel_id=2, replica_groups=mesh['sen'=32,'par'=16] {'sen'}, dimensions={0}, use_global_device_ids=true | all-gather | bytes 405504 | tf_op jit(solution)/shard_map/all_gather | solution.py:56
  372.5 62.8 %psum.14 = f32[2,8,256]{2,1,0:T(8,128)S(1)} all-reduce(f32[2,8,256]{2,1,0:T(8,128)S(1)} %copy_bitcast_fusion.3), channel_id=1, replica_groups=mesh['sen'=32,'par'=16] {'par'}, use_global_device_ids=true, to_apply=%region_1.2 | all-reduce | flops 4096 | bytes 32768 | tf_op jit(solution)/shard_map/psum | solution.py:65
  438.6 1.4 reshape.53
  440.0 219.5 %reduce-scatter.5.cloned.1.call-done = f32[16,384]{1,0:T(8,128)} async-done(((f32[512,384]{1,0:T(8,128)}), f32[16,384]{1,0:T(8,128)}) %reduce-scatter.5.cloned.1.call-update) | async-done | bytes 24592 | tf_op jit(solution)/shard_map/reduce_scatter | solution.py:52
  659.5 0.8 copy.82
  660.3 15.4 %all_to_all.48 = f32[16,1,384]{2,1,0:T(1,128)S(1)} all-to-all(f32[16,1,384]{2,1,0:T(1,128)S(1)} %copy.82), channel_id=1, replica_groups=mesh['sen'=32,'par'=16] {'par'}, dimensions={0} | all-to-all | bytes 49152 | tf_op jit(solution)/shard_map/all_to_all | solution.py:53
  676.3 0.6 reduce.1
  677.0 8.6 %all_to_all.49 = bf16[16,2,192]{2,1,0:T(2,128)(2,1)S(1)} all-to-all(bf16[16,2,192]{2,1,0:T(2,128)(2,1)S(1)} %reshape.82), channel_id=1, replica_groups=mesh['sen'=32,'par'=16] {'par'}, dimensions={0} | all-to-all | bytes 24576 | tf_op jit(solution)/shard_map/all_to_all | solution.py:55
  685.8 67.6 %all-gather.1 = bf16[512,1,384]{2,0,1:T(8,128)(2,1)S(1)} all-gather(bf16[16,1,384]{2,0,1:T(8,128)(2,1)S(1)} %copy.84), channel_id=3, replica_groups=mesh['sen'=32,'par'=16] {'sen'}, dimensions={0}, use_global_device_ids=true | all-gather | bytes 405504 | tf_op jit(solution)/shard_map/all_gather | solution.py:56
  755.7 62.8 %psum.15 = f32[2,8,256]{2,1,0:T(8,128)S(1)} all-reduce(f32[2,8,256]{2,1,0:T(8,128)S(1)} %copy_bitcast_fusion.2), channel_id=1, replica_groups=mesh['sen'=32,'par'=16] {'par'}, use_global_device_ids=true, to_apply=%region_3.4 | all-reduce | flops 4096 | bytes 32768 | tf_op jit(solution)/shard_map/psum | solution.py:65
  818.4 0.9 convolution_add_fusion.4
  (79 shorter events, 12.1 us)
Async XLA Ops:
  7.2 3.3 copy-start
  7.2 236.1 %reduce-scatter.3.cloned.1.call-start = ((), (), s32[]{:S(2)}) async-start(), calls=%async_computation.6 | async-start | bytes 811008 | tf_op jit(solution)/shard_map/reduce_scatter | solution.py:52
  12.4 242.1 %copy-start.5 = (f32[1,384]{1,0:T(1,128)S(1)}, f32[1,384]{1,0:T(1,128)}, u32[]{:S(2)}) copy-start(f32[1,384]{1,0:T(1,128)} %param.10) | copy-start | bytes 4612
  12.4 262.1 %copy-start.6 = (s32[1,384]{1,0:T(1,128)S(1)}, s32[1,384]{1,0:T(1,128)}, u32[]{:S(2)}) copy-start(s32[1,384]{1,0:T(1,128)} %param.11) | copy-start | bytes 4612
  244.7 46.1 %all-to-all-start = ((f32[16,1,384]{2,1,0:T(1,128)}), f32[16,1,384]{2,1,0:T(1,128)S(1)}, u32[]{:S(2)}, u32[]{:S(2)}) async-start(f32[16,1,384]{2,1,0:T(1,128)} %copy.61), calls=%async_computation.1 | async-start | bytes 49152 | tf_op jit(solution)/shard_map/all_to_all | solution.py:53
  293.3 9.3 %all-to-all-start.1 = ((bf16[16,2,192]{2,1,0:T(2,128)(2,1)}), bf16[16,2,192]{2,1,0:T(2,128)(2,1)S(1)}, u32[]{:S(2)}, u32[]{:S(2)}) async-start(bf16[16,2,192]{2,1,0:T(2,128)(2,1)} %reshape.80), calls=%async_computation.2 | async-start | bytes 32768 | tf_op jit(solution)/shard_map/all_to_all | solution.py:55
  296.7 362.8 %reduce-scatter.5.cloned.1.call-start = ((), (), s32[]{:S(2)}) async-start(), calls=%async_computation.7 | async-start | bytes 811008 | tf_op jit(solution)/shard_map/reduce_scatter | solution.py:52
  371.9 63.4 %copy-start.2 = (f32[2,8,256]{2,1,0:T(8,128)S(1)}, f32[2,8,256]{2,1,0:T(8,128)}, u32[]{:S(2)}) copy-start(f32[2,8,256]{2,1,0:T(8,128)} %param.6) | copy-start | bytes 49156
  371.9 63.4 %copy-start.3 = (f32[2,8,256]{2,1,0:T(8,128)S(1)}, f32[2,8,256]{2,1,0:T(8,128)}, u32[]{:S(2)}) copy-start(f32[2,8,256]{2,1,0:T(8,128)} %param.7) | copy-start | bytes 49156
  371.9 63.4 %copy-start.4 = (f32[8]{0:T(128)S(1)}, f32[8]{0:T(128)}, u32[]{:S(2)}) copy-start(f32[8]{0:T(128)} %param.9) | copy-start | bytes 100
  435.6 382.8 %copy-start.1 = (f32[2,8,256]{2,1,0:T(8,128)}, f32[2,8,256]{2,1,0:T(8,128)S(1)}, u32[]{:S(2)}) copy-start(f32[2,8,256]{2,1,0:T(8,128)S(1)} %fusion.8) | copy-start | bytes 49156
Sparse Core Ops, SparseCore 0:
  14.0 229.2 reduce-scatter.2
  440.2 219.3 reduce-scatter.4

commit v2 on v1

v2 whole, which is shorter than its diff:
```python
import math

import jax
import jax.numpy as jnp
import numpy as np
from jax import lax
from jax.experimental import pallas as pl
from jax.experimental.pallas import tpu as pltpu
from jax.sharding import PartitionSpec as P

SWEEPS = 4
NY, NZH, NX, NZL = 8, 4, 4, 2
NZ = NZH * NZL
SLAB = NY * NZ * 2
F32, BF16 = jnp.float32, jnp.bfloat16


def basis_rows(length):
    half = length // 2
    freqs = np.arange(half)[:, None]
    times = np.arange(length)[None, :]
    angle = ((2 * freqs + 1) * times % (2 * length)) * (math.pi / length)
    scale = math.sqrt(2.0 / length)
    return np.concatenate([np.cos(angle) * scale, np.sin(angle) * scale], 1).astype(np.float32)


def dot_rows(a, b, **kw):
    return lax.dot_general(a, b, (((1,), (1,)), ((), ())), preferred_element_type=F32, **kw)


def kernel(
    vec_ref, obs_ref, op_ref, noise_ref, coef_ref, offs_ref, basis_ref,
    res_ref, app_ref,
    w_buf, spec_own, spec_buf, co_buf, halo, sums, out_own, out_buf,
    op_send, op_recv, op_local, spec_send, spec_recv, row_send, row_recv, co_send, co_recv,
    halo_send, halo_recv, sum_send, sum_recv, out_send, out_recv,
):
    sen = lax.axis_index("sen")
    par = lax.axis_index("par")
    y, zh = lax.div(sen, NZH), lax.rem(sen, NZH)
    x, q_me = lax.div(par, 4), lax.rem(par, 4)
    zl, c = lax.div(q_me, 2), lax.rem(q_me, 2)
    z = zh * NZL + zl
    f_me = (y * NZ + z) * 2 + c

    def peer(k):
        dy = lax.rem(k, NY)
        dz = lax.rem(lax.div(k, NY) + 3 * dy, NZ)
        dc = lax.div(k, NY * NZ)
        y2 = lax.rem(y + dy, NY)
        z2 = lax.rem(z + dz, NZ)
        c2 = lax.rem(c + dc, 2)
        sen2 = y2 * NZH + lax.div(z2, NZL)
        par2 = x * 4 + lax.rem(z2, NZL) * 2 + c2
        return (y2 * NZ + z2) * 2 + c2, dc, sen2, par2

    def at(sen2, par2):
        return {"sen": sen2, "par": par2}

    def in_x(dx):
        return at(sen, lax.rem(x + dx, NX) * 4 + q_me)

    def remote(src, dst, send, recv, device):
        copy = pltpu.make_async_remote_copy(
            src_ref=src, dst_ref=dst, send_sem=send, recv_sem=recv,
            device_id=device, device_id_type=pl.DeviceIdType.MESH,
        )
        copy.start()

    def take(ref, sem):
        pltpu.make_async_copy(ref, ref, sem).wait()

    barrier = pltpu.get_barrier_semaphore()

    def greet(k, carry):
        _, _, sen2, par2 = peer(k)
        pl.semaphore_signal(barrier, inc=1, device_id=at(sen2, par2), device_id_type=pl.DeviceIdType.MESH)
        return carry

    lax.fori_loop(1, SLAB, greet, 0)
    for dx in range(1, NX):
        pl.semaphore_signal(barrier, inc=1, device_id=in_x(dx), device_id_type=pl.DeviceIdType.MESH)

    own_op = pltpu.make_async_copy(op_ref.at[:, f_me], w_buf.at[c, zl, :, sen], op_local)
    own_op.start()

    eye = lax.broadcasted_iota(jnp.int32, (8, 8), 0) == lax.broadcasted_iota(jnp.int32, (8, 8), 1)
    noise = jnp.sum(jnp.where(eye, noise_ref[...], 0.0), axis=1, keepdims=True)
    noise16 = jnp.concatenate([noise, noise], axis=0)
    vec = vec_ref[...].reshape(16, 256)
    rest = obs_ref[...].reshape(16, 256) - noise16 * vec
    record = jnp.concatenate([vec, rest], axis=0)
    blank = jnp.zeros_like(record)
    both = jnp.concatenate(
        [jnp.concatenate([record, blank], 1), jnp.concatenate([blank, record], 1), jnp.zeros((64, 512), F32)], 0
    )
    spec_own[...] = dot_rows(basis_ref[...], both, precision=lax.Precision.HIGHEST)

    co_buf[1, q_me, :, 0:384] = coef_ref[...]
    co_buf[1, q_me, :, 384:768] = offs_ref[...].astype(F32)

    pl.semaphore_wait(barrier, SLAB - 1 + NX - 1)

    def send_spec(k, carry):
        y2 = lax.rem(y + lax.rem(k, NY), NY)
        zh2 = lax.rem(zh + lax.div(k, NY), NZH)
        block = (y2 * NZ + zh2 * NZL) // 4
        rows = pl.ds(pl.multiple_of(block * 8, 8), 8)
        remote(spec_own.at[rows], spec_buf.at[sen], spec_send, spec_recv, at(y2 * NZH + zh2, par))
        return carry

    lax.fori_loop(1, NY * NZH, send_spec, 0)

    for dq in range(1, 4):
        q2 = lax.rem(q_me + dq, 4)
        zl2, c2 = lax.div(q2, 2), lax.rem(q2, 2)
        remote(co_buf.at[1, q_me], co_buf.at[1, q_me], row_send, row_recv, at(sen, x * 4 + zl2 * 2 + c2))

    def send_op(k, carry):
        f2, dc, sen2, par2 = peer(k)
        remote(op_ref.at[:, f2], w_buf.at[c, zl, :, sen], op_send, op_recv.at[dc], at(sen2, par2))
        return carry

    lax.fori_loop(1, SLAB, send_op, 0)

    take(co_buf.at[1, pl.ds(0, 3)], row_recv)
    remote(co_buf.at[1], co_buf.at[0], co_send.at[0], co_recv.at[0], in_x(1))
    remote(co_buf.at[1], co_buf.at[2], co_send.at[1], co_recv.at[1], in_x(NX - 1))
    take(co_buf.at[0], co_recv.at[0])
    take(co_buf.at[2], co_recv.at[1])
    above, below = x > 0, x < NX - 1

    def rows_of(first):
        parts = []
        for b in range(3):
            for r in range(4):
                row = jnp.broadcast_to(co_buf[b, r, :, first : first + 384], (4, 384))
                if b == 0:
                    row = jnp.where(above, row, 0.0)
                if b == 2:
                    row = jnp.where(below, row, 0.0)
                parts.append(row)
        return jnp.concatenate(parts, axis=0)

    coef = rows_of(0)
    column = lax.broadcasted_iota(jnp.int32, (48, 384), 1)
    offs = rows_of(384).astype(jnp.int32)
    landed = column + offs
    offs = jnp.where((landed >= 0) & (landed < 384), offs, 99)

    def smooth(field):
        for _ in range(SWEEPS):
            upper = pltpu.roll(field, 4, 0)
            lower = pltpu.roll(field, 44, 0)
            linked = jnp.zeros_like(field)
            for shift in range(-3, 4):
                moved = lower if shift == 0 else pltpu.roll(lower, (-shift) % 384, 1)
                linked = jnp.where(offs == shift, moved, linked)
            left = jnp.where(column == 0, 0.0, pltpu.roll(field, 1, 1))
            right = jnp.where(column == 383, 0.0, pltpu.roll(field, 383, 1))
            field = field + coef * (left + right + upper + linked - 4.0 * field)
        return field

    take(spec_buf.at[pl.ds(0, NY * NZH - 1)], spec_recv)
    mine = pl.ds(pl.multiple_of(lax.div(f_me, 8) * 8, 8), 8)
    spec_buf[sen] = spec_own[mine, :]
    pick = lax.broadcasted_iota(jnp.int32, (32, 8, 128), 1) == lax.rem(f_me, 8)
    gathered = jnp.sum(jnp.where(pick, spec_buf[...], 0.0), axis=1)
    lane = lax.broadcasted_iota(jnp.int32, (32, 128), 1)
    sensor_row = lax.broadcasted_iota(jnp.int32, (32, 256), 0)
    sensor_lane = lax.broadcasted_iota(jnp.int32, (32, 256), 1) // 8
    whole = []
    for q in range(8):
        piece = jnp.where(lane // 8 == q, gathered, 0.0)
        for shift in (8, 16, 32, 64):
            piece = piece + pltpu.roll(piece, shift, 1)
        piece = jnp.concatenate([piece, piece], axis=1)
        whole.append(jnp.sum(jnp.where(sensor_row == sensor_lane, piece, 0.0), axis=0, keepdims=True))

    def stack(re, im):
        re, im = re.astype(BF16).astype(F32), im.astype(BF16).astype(F32)
        return jnp.concatenate(
            [jnp.concatenate([re, im], 1), jnp.concatenate([im, -re], 1)], 0
        ).astype(BF16)

    def weights(core, low):
        return w_buf[core, low].reshape(512, 384)

    def adjoint_of(h, spectra, core):
        for low in range(2):
            halo[h, 1, low * 2 + core] = jnp.dot(spectra, weights(core, low), preferred_element_type=F32)

    def rest_of(h):
        remote(halo.at[h, 1], halo.at[h, 0], halo_send.at[h, 0], halo_recv.at[h, 0], in_x(1))
        remote(halo.at[h, 1], halo.at[h, 2], halo_send.at[h, 1], halo_recv.at[h, 1], in_x(NX - 1))
        take(halo.at[h, 0], halo_recv.at[h, 0])
        take(halo.at[h, 2], halo_recv.at[h, 1])
        parts = []
        for b in range(3):
            for r in range(4):
                row = halo[h, b, r]
                if b == 0:
                    row = jnp.where(above, row, 0.0)
                if b == 2:
                    row = jnp.where(below, row, 0.0)
                parts.append(row)
        smoothed = smooth(jnp.concatenate(parts, axis=0))
        total = jnp.zeros((4, 512), F32)
        for q in range(4):
            prior = smoothed[16 + 4 * q : 20 + 4 * q].astype(BF16)
            total = total + dot_rows(prior, weights(q % 2, q // 2))
        sums[h, x] = jnp.concatenate(
            [total[0:2, :256] - total[2:4, 256:], total[2:4, :256] + total[0:2, 256:]], 0
        )
        for dx in range(1, NX):
            remote(sums.at[h, x], sums.at[h, x], sum_send.at[h], sum_recv.at[h], in_x(dx))
        take(sums.at[h, pl.ds(0, NX - 1)], sum_recv.at[h])
        forward = ((sums[h, 0] + sums[h, 1]) + sums[h, 2]) + sums[h, 3]
        rows = jnp.zeros((32, 128), F32)
        for q in range(4):
            piece = jnp.where(sensor_row == sensor_lane, jnp.broadcast_to(forward[q : q + 1], (32, 256)), 0.0)
            piece = piece[:, :128] + piece[:, 128:]
            for shift in (8, 16, 32, 64):
                piece = piece + pltpu.roll(piece, shift, 1)
            rows = jnp.where(lane // 8 == q, piece, rows)
        out_own[h] = rows.reshape(32, 1, 128)

        def send_out(k, carry):
            _, _, sen2, par2 = peer(k)
            remote(out_own.at[h, sen2], out_buf.at[h, f_me], out_send.at[h], out_recv.at[h], at(sen2, par2))
            return carry

        lax.fori_loop(1, SLAB, send_out, 0)
        out_buf[h, f_me] = out_own[h, sen]
        return forward

    def back_of(h):
        take(out_buf.at[h, pl.ds(0, SLAB - 1)], out_recv.at[h])
        got = out_buf[h].reshape(128, 128)
        dims = (((0,), (0,)), ((), ()))
        even = lax.dot_general(got, basis_ref[:, :256], dims, preferred_element_type=F32, precision=lax.Precision.HIGHEST)
        odd = lax.dot_general(got, basis_ref[:, 256:], dims, preferred_element_type=F32, precision=lax.Precision.HIGHEST)
        return even[0:16] + odd[16:32]

    first = stack(jnp.concatenate(whole[0:2], 0), jnp.concatenate(whole[4:6], 0))
    own_op.wait()
    take(op_ref.at[:, pl.ds(0, SLAB // 2 - 1)], op_recv.at[0])
    adjoint_of(0, first, c)
    take(op_ref.at[:, pl.ds(0, SLAB // 2)], op_recv.at[1])
    adjoint_of(0, first, 1 - c)
    forward = rest_of(0)
    second = stack(
        jnp.concatenate(whole[2:4], 0) - forward[0:2], jnp.concatenate(whole[6:8], 0) - forward[2:4]
    )
    adjoint_of(1, second, c)
    adjoint_of(1, second, 1 - c)
    rest_of(1)
    residual = rest - back_of(0)
    res_ref[...] = residual.reshape(2, 8, 256)
    app_ref[...] = (back_of(1) + noise16 * residual).reshape(2, 8, 256)

    take(op_ref.at[:, pl.ds(0, SLAB - 1)], op_send)
    take(spec_buf.at[pl.ds(0, NY * NZH - 1)], spec_send)
    take(co_buf.at[1, pl.ds(0, 3)], row_send)
    take(co_buf.at[0], co_send.at[0])
    take(co_buf.at[2], co_send.at[1])
    for h in range(2):
        take(halo.at[h, 0], halo_send.at[h, 0])
        take(halo.at[h, 2], halo_send.at[h, 1])
        take(sums.at[h, pl.ds(0, NX - 1)], sum_send.at[h])
        take(out_buf.at[h, pl.ds(0, SLAB - 1)], out_send.at[h])


def body(vectors, observed, operator, noise, coefficient, offsets):
    vmem = pl.BlockSpec(memory_space=pltpu.VMEM)
    dma = pltpu.SemaphoreType.DMA
    return pl.pallas_call(
        kernel,
        out_shape=(jax.ShapeDtypeStruct(vectors.shape, F32),) * 2,
        in_specs=[vmem, vmem, pl.BlockSpec(memory_space=pl.ANY), vmem, vmem, vmem, vmem],
        out_specs=(vmem, vmem),
        scratch_shapes=[
            pltpu.VMEM((2, 2, 2, 32, 8, 384), BF16),
            pltpu.VMEM((128, 128), F32),
            pltpu.VMEM((32, 8, 128), F32),
            pltpu.VMEM((3, 4, 1, 768), F32),
            pltpu.VMEM((2, 3, 4, 4, 384), F32),
            pltpu.VMEM((2, 4, 4, 256), F32),
            pltpu.VMEM((2, 32, 1, 128), F32),
            pltpu.VMEM((2, 128, 1, 128), F32),
            dma, dma((2,)), dma, dma, dma, dma, dma, dma((2,)), dma((2,)),
            dma((2, 2)), dma((2, 2)), dma((2,)), dma((2,)), dma((2,)), dma((2,)),
        ],
        compiler_params=pltpu.CompilerParams(
            collective_id=0, has_side_effects=True, vmem_limit_bytes=32 * 1024 * 1024
        ),
    )(vectors, observed, operator, noise.reshape(1, 8), coefficient, offsets, jnp.asarray(basis_rows(256)))


def solution(mesh):
    placed = (
        P(None, "sen", None),
        P(None, "sen", None),
        P(None, None, "sen", "par"),
        P("sen"),
        P("par", None),
        P("par", None),
    )
    return jax.shard_map(
        body,
        mesh=mesh,
        in_specs=placed,
        out_specs=(P(None, "sen", None), P(None, "sen", None)),
        check_vma=False,
    )
```

time: 827 us -> 102 us (0.12)
  waiting for transfers between devices: 455 us -> 0 us
  blocking collectives: 321 us -> 0 us
  Pallas kernels: 0 us -> 94.2 us
  between operations: 14.4 us -> 0.65 us
  starting transfers between devices: 13.3 us -> 0 us
  matrix products: 11.1 us -> 0 us
    reduce_scatter x2 -> x0, waiting for transfers between devices: 449 us -> none  [hessian(): planes = lax.psum_scatter(planes, 'sen', scatter_dimension=0, tiled=True)]
    all_gather x4 -> x0, blocking collectives: 171 us -> none  [the longest x2 135 us: hessian(): planes = lax.all_gather(planes, 'sen', axis=0, tiled=True)]
    psum x2 -> x0, blocking collectives: 126 us -> none  [hessian(): forward = lax.psum(jnp.stack([real, imag]), 'par')]
    pallas_call x0 -> x1, Pallas kernels: none -> 94.2 us  [body(): pl.pallas_call(kernel, out_shape=(jax.ShapeDtypeStruct(vectors.shape, F32...]
    all_to_all x2 -> x0, blocking collectives: 24 us -> none  [the longest x1 15.4 us: hessian(): plane = lax.all_to_all(planes, 'par', 0, 0, tiled=True)]
    all_to_all x2 -> x0, starting transfers between devices: 13.3 us -> none  [the longest x1 9.82 us: hessian(): plane = lax.all_to_all(planes, 'par', 0, 0, tiled=True)]
    dot_general x20 -> x0, matrix products: 11.1 us -> none  [the longest x2 1.97 us: hessian(): jnp.einsum('frs,fsp->frp', spectrum[0], operator[0], preferred_element_ty...]
  transfers between devices with their start and end apart: 4 -> 0, of which waited for: 3 -> 0; matrix products, arithmetic and copies ran while one was open for 0% -> 0% of each run, Pallas kernels for 0% -> 0%
where the time goes in v2:
time: 102 us
  Pallas kernels  94.2 us (92%)
  local copies, waits for them, and re-layouts  7.01 us (7%)
    pallas_call x1, Pallas kernels, body(): pl.pallas_call(kernel, out_shape=(jax.ShapeDtypeStruct(vectors.shape, F32...  94.2 us
    unnamed x16, local copies, waits for them, and re-layouts  7.01 us

profile of v2, /device:TPU:1, one launch (start us, length us, event | category | flops | bytes accessed | tf_op | source)
XLA Modules:
  0.0 101.9 jit_solution(5370177371810567719)
XLA Ops:
  0.6 0.0 copy-start
  0.6 1.4 %copy-done = bf16[2,128,8,384]{3,2,1,0:T(8,128)(2,1)S(1)} copy-done((bf16[2,128,8,384]{3,2,1,0:T(8,128)(2,1)S(1)}, bf16[2,128,8,384]{3,2,1,0:T(8,128)(2,1)}, u32[]{:S(2)}) %copy-start) | copy-done | bytes 1572888
  2.0 0.0 copy-start.1
  2.0 0.9 copy-done.1
  3.0 0.0 copy-start.2
  3.0 0.7 copy-done.2
  3.7 0.0 copy-start.3
  3.7 0.7 copy-done.3
  4.4 0.0 copy-start.4
  4.4 0.7 copy-done.4
  5.1 0.0 copy-start.5
  5.1 0.7 copy-done.5
  5.8 0.0 copy-start.6
  5.8 0.7 copy-done.6
  6.4 94.2 %shard_map.86 = (f32[2,8,256]{2,1,0:T(8,128)S(1)}, f32[2,8,256]{2,1,0:T(8,128)S(1)}) custom-call(f32[2,8,256]{2,1,0:T(8,128)S(1)} %copy-done.2, f32[2,8,256]{2,1,0:T(8,128)S(1)} %copy-done.3, bf16[2,128,8,384]{3,2,1,0:T(8,128)(2,1)S(1)} %copy-done, f32[1,8]{1,0:T(1,128)S(1)} %bitcast.1, f32[1,384]{1,0:T(1,128)S(1)} %copy-done.4, s32[1,384]{1,0:T(1,128)S(1)} %copy-done.5, ...), custom_call_target="tpu_custom_call" | custom-call | tf_op jit(solution)/shard_map/pallas_call | solution.py:277
  100.6 0.6 copy.11
  101.3 0.6 copy.12
Async XLA Ops:
  0.6 1.4 %copy-start = (bf16[2,128,8,384]{3,2,1,0:T(8,128)(2,1)S(1)}, bf16[2,128,8,384]{3,2,1,0:T(8,128)(2,1)}, u32[]{:S(2)}) copy-start(bf16[2,128,8,384]{3,2,1,0:T(8,128)(2,1)} %op_ref.1) | copy-start | bytes 4718596
  2.0 0.9 copy-start.1
  3.0 0.7 copy-start.2
  3.7 0.7 copy-start.3
  4.4 0.7 copy-start.4
  5.1 0.7 copy-start.5
  5.8 0.7 copy-start.6

commit v3 on v2

--- a/solution.py
+++ b/solution.py
@@ -12,6 +12,7 @@
 NY, NZH, NX, NZL = 8, 4, 4, 2
 NZ = NZH * NZL
 SLAB = NY * NZ * 2
+STRIDE = 37
 F32, BF16 = jnp.float32, jnp.bfloat16
 
 
@@ -29,30 +30,23 @@
 
 
 def kernel(
-    vec_ref, obs_ref, op_ref, noise_ref, coef_ref, offs_ref, basis_ref,
+    vec_hbm, obs_hbm, op_ref, noise_hbm, coef_hbm, offs_hbm, basis_hbm,
     res_ref, app_ref,
+    vec_ref, obs_ref, noise_ref, coef_ref, offs_ref, basis_ref,
     w_buf, spec_own, spec_buf, co_buf, halo, sums, out_own, out_buf,
-    op_send, op_recv, op_local, spec_send, spec_recv, row_send, row_recv, co_send, co_recv,
+    load_sem, op_send, op_recv, op_local, spec_send, spec_recv, row_send, row_recv, co_send, co_recv,
     halo_send, halo_recv, sum_send, sum_recv, out_send, out_recv,
 ):
     sen = lax.axis_index("sen")
     par = lax.axis_index("par")
-    y, zh = lax.div(sen, NZH), lax.rem(sen, NZH)
     x, q_me = lax.div(par, 4), lax.rem(par, 4)
     zl, c = lax.div(q_me, 2), lax.rem(q_me, 2)
-    z = zh * NZL + zl
-    f_me = (y * NZ + z) * 2 + c
+    f_me = sen * 4 + q_me
 
     def peer(k):
-        dy = lax.rem(k, NY)
-        dz = lax.rem(lax.div(k, NY) + 3 * dy, NZ)
-        dc = lax.div(k, NY * NZ)
-        y2 = lax.rem(y + dy, NY)
-        z2 = lax.rem(z + dz, NZ)
-        c2 = lax.rem(c + dc, 2)
-        sen2 = y2 * NZH + lax.div(z2, NZL)
-        par2 = x * 4 + lax.rem(z2, NZL) * 2 + c2
-        return (y2 * NZ + z2) * 2 + c2, dc, sen2, par2
+        late = k // (SLAB // 2)
+        f2 = lax.rem(f_me + STRIDE * (2 * k - (SLAB - 1) * late), SLAB)
+        return f2, late, lax.div(f2, 4), par - q_me + lax.rem(f2, 4)
 
     def at(sen2, par2):
         return {"sen": sen2, "par": par2}
@@ -70,6 +64,14 @@
     def take(ref, sem):
         pltpu.make_async_copy(ref, ref, sem).wait()
 
+    loads = []
+    for i, (src, dst) in enumerate(
+        ((vec_hbm, vec_ref), (obs_hbm, obs_ref), (noise_hbm, noise_ref),
+         (coef_hbm, coef_ref), (offs_hbm, offs_ref), (basis_hbm, basis_ref))
+    ):
+        loads.append(pltpu.make_async_copy(src, dst, load_sem.at[i]))
+        loads[-1].start()
+
     barrier = pltpu.get_barrier_semaphore()
 
     def greet(k, carry):
@@ -84,6 +86,8 @@
     own_op = pltpu.make_async_copy(op_ref.at[:, f_me], w_buf.at[c, zl, :, sen], op_local)
     own_op.start()
 
+    for load in loads:
+        load.wait()
     eye = lax.broadcasted_iota(jnp.int32, (8, 8), 0) == lax.broadcasted_iota(jnp.int32, (8, 8), 1)
     noise = jnp.sum(jnp.where(eye, noise_ref[...], 0.0), axis=1, keepdims=True)
     noise16 = jnp.concatenate([noise, noise], axis=0)
@@ -102,11 +106,9 @@
     pl.semaphore_wait(barrier, SLAB - 1 + NX - 1)
 
     def send_spec(k, carry):
-        y2 = lax.rem(y + lax.rem(k, NY), NY)
-        zh2 = lax.rem(zh + lax.div(k, NY), NZH)
-        block = (y2 * NZ + zh2 * NZL) // 4
-        rows = pl.ds(pl.multiple_of(block * 8, 8), 8)
-        remote(spec_own.at[rows], spec_buf.at[sen], spec_send, spec_recv, at(y2 * NZH + zh2, par))
+        sen2 = lax.rem(sen + 11 * k, NY * NZH)
+        rows = pl.ds(pl.multiple_of(lax.div(sen2, 2) * 8, 8), 8)
+        remote(spec_own.at[rows], spec_buf.at[sen], spec_send, spec_recv, at(sen2, par))
         return carry
 
     lax.fori_loop(1, NY * NZH, send_spec, 0)
@@ -216,31 +218,34 @@
             remote(sums.at[h, x], sums.at[h, x], sum_send.at[h], sum_recv.at[h], in_x(dx))
         take(sums.at[h, pl.ds(0, NX - 1)], sum_recv.at[h])
         forward = ((sums[h, 0] + sums[h, 1]) + sums[h, 2]) + sums[h, 3]
+        return forward
+
+    def send_outs(forwards):
         rows = jnp.zeros((32, 128), F32)
-        for q in range(4):
-            piece = jnp.where(sensor_row == sensor_lane, jnp.broadcast_to(forward[q : q + 1], (32, 256)), 0.0)
+        for q in range(8):
+            row = forwards[q // 4][q % 4 : q % 4 + 1]
+            piece = jnp.where(sensor_row == sensor_lane, jnp.broadcast_to(row, (32, 256)), 0.0)
             piece = piece[:, :128] + piece[:, 128:]
             for shift in (8, 16, 32, 64):
                 piece = piece + pltpu.roll(piece, shift, 1)
             rows = jnp.where(lane // 8 == q, piece, rows)
-        out_own[h] = rows.reshape(32, 1, 128)
+        out_own[...] = rows.reshape(32, 1, 128)
 
         def send_out(k, carry):
             _, _, sen2, par2 = peer(k)
-            remote(out_own.at[h, sen2], out_buf.at[h, f_me], out_send.at[h], out_recv.at[h], at(sen2, par2))
+            remote(out_own.at[sen2], out_buf.at[f_me], out_send, out_recv, at(sen2, par2))
             return carry
 
         lax.fori_loop(1, SLAB, send_out, 0)
-        out_buf[h, f_me] = out_own[h, sen]
-        return forward
-
-    def back_of(h):
-        take(out_buf.at[h, pl.ds(0, SLAB - 1)], out_recv.at[h])
-        got = out_buf[h].reshape(128, 128)
+        out_buf[f_me] = out_own[sen]
+
+    def backs():
+        take(out_buf.at[pl.ds(0, SLAB - 1)], out_recv)
+        got = out_buf[...].reshape(128, 128)
         dims = (((0,), (0,)), ((), ()))
         even = lax.dot_general(got, basis_ref[:, :256], dims, preferred_element_type=F32, precision=lax.Precision.HIGHEST)
         odd = lax.dot_general(got, basis_ref[:, 256:], dims, preferred_element_type=F32, precision=lax.Precision.HIGHEST)
-        return even[0:16] + odd[16:32]
+        return even[0:16] + odd[16:32], even[32:48] + odd[48:64]
 
     first = stack(jnp.concatenate(whole[0:2], 0), jnp.concatenate(whole[4:6], 0))
     own_op.wait()
@@ -254,10 +259,11 @@
     )
     adjoint_of(1, second, c)
     adjoint_of(1, second, 1 - c)
-    rest_of(1)
-    residual = rest - back_of(0)
+    send_outs((forward, rest_of(1)))
+    back_0, back_1 = backs()
+    residual = rest - back_0
     res_ref[...] = residual.reshape(2, 8, 256)
-    app_ref[...] = (back_of(1) + noise16 * residual).reshape(2, 8, 256)
+    app_ref[...] = (back_1 + noise16 * residual).reshape(2, 8, 256)
 
     take(op_ref.at[:, pl.ds(0, SLAB - 1)], op_send)
     take(spec_buf.at[pl.ds(0, NY * NZH - 1)], spec_send)
@@ -268,7 +274,7 @@
         take(halo.at[h, 0], halo_send.at[h, 0])
         take(halo.at[h, 2], halo_send.at[h, 1])
         take(sums.at[h, pl.ds(0, NX - 1)], sum_send.at[h])
-        take(out_buf.at[h, pl.ds(0, SLAB - 1)], out_send.at[h])
+    take(out_buf.at[pl.ds(0, SLAB - 1)], out_send)
 
 
 def body(vectors, observed, operator, noise, coefficient, offsets):
@@ -277,22 +283,28 @@
     return pl.pallas_call(
         kernel,
         out_shape=(jax.ShapeDtypeStruct(vectors.shape, F32),) * 2,
-        in_specs=[vmem, vmem, pl.BlockSpec(memory_space=pl.ANY), vmem, vmem, vmem, vmem],
+        in_specs=[pl.BlockSpec(memory_space=pl.ANY)] * 7,
         out_specs=(vmem, vmem),
         scratch_shapes=[
+            pltpu.VMEM((2, 8, 256), F32),
+            pltpu.VMEM((2, 8, 256), F32),
+            pltpu.VMEM((1, 8), F32),
+            pltpu.VMEM((1, 384), F32),
+            pltpu.VMEM((1, 384), jnp.int32),
+            pltpu.VMEM((128, 512), F32),
             pltpu.VMEM((2, 2, 2, 32, 8, 384), BF16),
             pltpu.VMEM((128, 128), F32),
             pltpu.VMEM((32, 8, 128), F32),
             pltpu.VMEM((3, 4, 1, 768), F32),
             pltpu.VMEM((2, 3, 4, 4, 384), F32),
             pltpu.VMEM((2, 4, 4, 256), F32),
-            pltpu.VMEM((2, 32, 1, 128), F32),
-            pltpu.VMEM((2, 128, 1, 128), F32),
-            dma, dma((2,)), dma, dma, dma, dma, dma, dma((2,)), dma((2,)),
-            dma((2, 2)), dma((2, 2)), dma((2,)), dma((2,)), dma((2,)), dma((2,)),
+            pltpu.VMEM((32, 1, 128), F32),
+            pltpu.VMEM((128, 1, 128), F32),
+            dma((6,)), dma, dma((2,)), dma, dma, dma, dma, dma, dma((2,)), dma((2,)),
+            dma((2, 2)), dma((2, 2)), dma((2,)), dma((2,)), dma, dma,
         ],
         compiler_params=pltpu.CompilerParams(
-            collective_id=0, has_side_effects=True, vmem_limit_bytes=32 * 1024 * 1024
+            collective_id=0, has_side_effects=True, vmem_limit_bytes=60 * 1024 * 1024
         ),
     )(vectors, observed, operator, noise.reshape(1, 8), coefficient, offsets, jnp.asarray(basis_rows(256)))
 

time: 102 us -> 93 us (0.912)
  Pallas kernels: 94.2 us -> 89.4 us
  local copies, waits for them, and re-layouts: 7.01 us -> 2.65 us
    pallas_call x1, Pallas kernels: 94.2 us -> 89.4 us  [body(): pl.pallas_call(kernel, out_shape=(jax.ShapeDtypeStruct(vectors.shape, F32...]
    unnamed x16 -> x2, local copies, waits for them, and re-layouts: 7.01 us -> 2.65 us
where the time goes in v3:
time: 93 us; the launch traced here: 92.7 us
  Pallas kernels  89.4 us (96%)
  local copies, waits for them, and re-layouts  2.65 us (3%)
    pallas_call x1, Pallas kernels, body(): pl.pallas_call(kernel, out_shape=(jax.ShapeDtypeStruct(vectors.shape, F32...  89.4 us
    unnamed x2, local copies, waits for them, and re-layouts  2.65 us

profile of v3, /device:TPU:1, one launch (start us, length us, event | category | flops | bytes accessed | tf_op | source)
XLA Modules:
  0.0 92.7 jit_solution(17684796823761303272)
XLA Ops:
  0.6 89.4 %shard_map.86 = (f32[2,8,256]{2,1,0:T(8,128)}, f32[2,8,256]{2,1,0:T(8,128)}) custom-call(f32[2,8,256]{2,1,0:T(8,128)} %vec_hbm.1, f32[2,8,256]{2,1,0:T(8,128)} %obs_hbm.1, bf16[2,128,8,384]{3,2,1,0:T(8,128)(2,1)} %op_ref.1, f32[1,8]{1,0:T(1,128)} %bitcast.1, f32[1,384]{1,0:T(1,128)} %coef_hbm.1, s32[1,384]{1,0:T(1,128)} %offs_hbm.1, ...), custom_call_target="tpu_custom_call" | custom-call | tf_op jit(solution)/shard_map/pallas_call | solution.py:283
  90.0 1.3 %copy.11 = f32[2,8,256]{2,1,0:T(8,128)} copy(f32[2,8,256]{2,1,0:T(8,128)} %get-tuple-element.4) | data formatting | bytes 32768
  91.3 1.3 %copy.12 = f32[2,8,256]{2,1,0:T(8,128)} copy(f32[2,8,256]{2,1,0:T(8,128)} %get-tuple-element.5) | data formatting | bytes 32768

commit v4 on v3

--- a/solution.py
+++ b/solution.py
@@ -43,21 +43,26 @@
     zl, c = lax.div(q_me, 2), lax.rem(q_me, 2)
     f_me = sen * 4 + q_me
 
-    def peer(k):
-        late = k // (SLAB // 2)
-        f2 = lax.rem(f_me + STRIDE * (2 * k - (SLAB - 1) * late), SLAB)
-        return f2, late, lax.div(f2, 4), par - q_me + lax.rem(f2, 4)
+    def wrap(value, size):
+        return jnp.where(value >= size, value - size, value)
 
     def at(sen2, par2):
-        return {"sen": sen2, "par": par2}
+        return sen2 * (4 * NX) + par2
 
     def in_x(dx):
-        return at(sen, lax.rem(x + dx, NX) * 4 + q_me)
+        return at(sen, wrap(x + dx, NX) * 4 + q_me)
+
+    def each_block(act):
+        def one(k, sen2):
+            act(sen2)
+            return wrap(sen2 + 11, NY * NZH)
+
+        lax.fori_loop(1, NY * NZH, one, wrap(sen + 11, NY * NZH))
 
     def remote(src, dst, send, recv, device):
         copy = pltpu.make_async_remote_copy(
             src_ref=src, dst_ref=dst, send_sem=send, recv_sem=recv,
-            device_id=device, device_id_type=pl.DeviceIdType.MESH,
+            device_id=device, device_id_type=pl.DeviceIdType.LOGICAL,
         )
         copy.start()
 
@@ -74,14 +79,18 @@
 
     barrier = pltpu.get_barrier_semaphore()
 
-    def greet(k, carry):
-        _, _, sen2, par2 = peer(k)
-        pl.semaphore_signal(barrier, inc=1, device_id=at(sen2, par2), device_id_type=pl.DeviceIdType.MESH)
-        return carry
-
-    lax.fori_loop(1, SLAB, greet, 0)
+    def tell(device):
+        pl.semaphore_signal(barrier, inc=1, device_id=device, device_id_type=pl.DeviceIdType.LOGICAL)
+
+    def greet(sen2):
+        for q2 in range(4):
+            tell(at(sen2, x * 4 + q2))
+
+    each_block(greet)
+    for dq in range(1, 4):
+        tell(at(sen, x * 4 + wrap(q_me + dq, 4)))
     for dx in range(1, NX):
-        pl.semaphore_signal(barrier, inc=1, device_id=in_x(dx), device_id_type=pl.DeviceIdType.MESH)
+        tell(in_x(dx))
 
     own_op = pltpu.make_async_copy(op_ref.at[:, f_me], w_buf.at[c, zl, :, sen], op_local)
     own_op.start()
@@ -105,43 +114,78 @@
 
     pl.semaphore_wait(barrier, SLAB - 1 + NX - 1)
 
-    def send_spec(k, carry):
-        sen2 = lax.rem(sen + 11 * k, NY * NZH)
+    def send_op(sen2, q2, core):
+        remote(op_ref.at[:, sen2 * 4 + q2], w_buf.at[c, zl, :, sen], op_send, op_recv.at[core], at(sen2, x * 4 + q2))
+
+    def send_core(core):
+        mine = jnp.where(core == 0, c, 1 - c)
+
+        def send_block(sen2):
+            for low in range(2):
+                send_op(sen2, low * 2 + mine, core)
+
+        each_block(send_block)
+        send_op(sen, (1 - zl) * 2 + mine, core)
+        if core == 1:
+            send_op(sen, zl * 2 + mine, core)
+
+    send_core(0)
+
+    def send_spec(sen2):
         rows = pl.ds(pl.multiple_of(lax.div(sen2, 2) * 8, 8), 8)
         remote(spec_own.at[rows], spec_buf.at[sen], spec_send, spec_recv, at(sen2, par))
-        return carry
-
-    lax.fori_loop(1, NY * NZH, send_spec, 0)
-
+
+    each_block(send_spec)
     for dq in range(1, 4):
-        q2 = lax.rem(q_me + dq, 4)
-        zl2, c2 = lax.div(q2, 2), lax.rem(q2, 2)
-        remote(co_buf.at[1, q_me], co_buf.at[1, q_me], row_send, row_recv, at(sen, x * 4 + zl2 * 2 + c2))
-
-    def send_op(k, carry):
-        f2, dc, sen2, par2 = peer(k)
-        remote(op_ref.at[:, f2], w_buf.at[c, zl, :, sen], op_send, op_recv.at[dc], at(sen2, par2))
-        return carry
-
-    lax.fori_loop(1, SLAB, send_op, 0)
+        remote(
+            co_buf.at[1, q_me], co_buf.at[1, q_me], row_send, row_recv, at(sen, x * 4 + wrap(q_me + dq, 4))
+        )
+    send_core(1)
 
     take(co_buf.at[1, pl.ds(0, 3)], row_recv)
-    remote(co_buf.at[1], co_buf.at[0], co_send.at[0], co_recv.at[0], in_x(1))
-    remote(co_buf.at[1], co_buf.at[2], co_send.at[1], co_recv.at[1], in_x(NX - 1))
-    take(co_buf.at[0], co_recv.at[0])
-    take(co_buf.at[2], co_recv.at[1])
     above, below = x > 0, x < NX - 1
+
+    def to_neighbours(buf, send, recv):
+        @pl.when(below)
+        def _():
+            remote(buf.at[1], buf.at[0], send.at[0], recv.at[0], par_at(x + 1))
+
+        @pl.when(above)
+        def _():
+            remote(buf.at[1], buf.at[2], send.at[1], recv.at[1], par_at(x - 1))
+
+    def from_neighbours(buf, recv):
+        @pl.when(above)
+        def _():
+            take(buf.at[0], recv.at[0])
+
+        @pl.when(below)
+        def _():
+            take(buf.at[2], recv.at[1])
+
+    def par_at(x2):
+        return at(sen, x2 * 4 + q_me)
+
+    def clear(buf):
+        @pl.when(x == 0)
+        def _():
+            buf[0] = jnp.zeros(buf.shape[1:], F32)
+
+        @pl.when(x == NX - 1)
+        def _():
+            buf[2] = jnp.zeros(buf.shape[1:], F32)
+
+    clear(co_buf)
+    for h in range(2):
+        clear(halo.at[h])
+    to_neighbours(co_buf, co_send, co_recv)
+    from_neighbours(co_buf, co_recv)
 
     def rows_of(first):
         parts = []
         for b in range(3):
             for r in range(4):
-                row = jnp.broadcast_to(co_buf[b, r, :, first : first + 384], (4, 384))
-                if b == 0:
-                    row = jnp.where(above, row, 0.0)
-                if b == 2:
-                    row = jnp.where(below, row, 0.0)
-                parts.append(row)
+                parts.append(jnp.broadcast_to(co_buf[b, r, :, first : first + 384], (4, 384)))
         return jnp.concatenate(parts, axis=0)
 
     coef = rows_of(0)
@@ -192,20 +236,11 @@
         for low in range(2):
             halo[h, 1, low * 2 + core] = jnp.dot(spectra, weights(core, low), preferred_element_type=F32)
 
-    def rest_of(h):
-        remote(halo.at[h, 1], halo.at[h, 0], halo_send.at[h, 0], halo_recv.at[h, 0], in_x(1))
-        remote(halo.at[h, 1], halo.at[h, 2], halo_send.at[h, 1], halo_recv.at[h, 1], in_x(NX - 1))
-        take(halo.at[h, 0], halo_recv.at[h, 0])
-        take(halo.at[h, 2], halo_recv.at[h, 1])
-        parts = []
-        for b in range(3):
-            for r in range(4):
-                row = halo[h, b, r]
-                if b == 0:
-                    row = jnp.where(above, row, 0.0)
-                if b == 2:
-                    row = jnp.where(below, row, 0.0)
-                parts.append(row)
+    def rest_of(h, meanwhile):
+        to_neighbours(halo.at[h], halo_send.at[h], halo_recv.at[h])
+        done = meanwhile()
+        from_neighbours(halo.at[h], halo_recv.at[h])
+        parts = [halo[h, b, r] for b in range(3) for r in range(4)]
         smoothed = smooth(jnp.concatenate(parts, axis=0))
         total = jnp.zeros((4, 512), F32)
         for q in range(4):
@@ -218,25 +253,27 @@
             remote(sums.at[h, x], sums.at[h, x], sum_send.at[h], sum_recv.at[h], in_x(dx))
         take(sums.at[h, pl.ds(0, NX - 1)], sum_recv.at[h])
         forward = ((sums[h, 0] + sums[h, 1]) + sums[h, 2]) + sums[h, 3]
-        return forward
-
-    def send_outs(forwards):
-        rows = jnp.zeros((32, 128), F32)
-        for q in range(8):
-            row = forwards[q // 4][q % 4 : q % 4 + 1]
-            piece = jnp.where(sensor_row == sensor_lane, jnp.broadcast_to(row, (32, 256)), 0.0)
+        return forward, done
+
+    def arrange(forward, rows, first):
+        for q in range(4):
+            piece = jnp.where(sensor_row == sensor_lane, jnp.broadcast_to(forward[q : q + 1], (32, 256)), 0.0)
             piece = piece[:, :128] + piece[:, 128:]
             for shift in (8, 16, 32, 64):
                 piece = piece + pltpu.roll(piece, shift, 1)
-            rows = jnp.where(lane // 8 == q, piece, rows)
+            rows = jnp.where(lane // 8 == first + q, piece, rows)
+        return rows
+
+    def send_outs(rows):
         out_own[...] = rows.reshape(32, 1, 128)
 
-        def send_out(k, carry):
-            _, _, sen2, par2 = peer(k)
-            remote(out_own.at[sen2], out_buf.at[f_me], out_send, out_recv, at(sen2, par2))
-            return carry
-
-        lax.fori_loop(1, SLAB, send_out, 0)
+        def send_out(sen2):
+            for q2 in range(4):
+                remote(out_own.at[sen2], out_buf.at[f_me], out_send, out_recv, at(sen2, x * 4 + q2))
+
+        each_block(send_out)
+        for dq in range(1, 4):
+            remote(out_own.at[sen], out_buf.at[f_me], out_send, out_recv, at(sen, x * 4 + wrap(q_me + dq, 4)))
         out_buf[f_me] = out_own[sen]
 
     def backs():
@@ -253,13 +290,14 @@
     adjoint_of(0, first, c)
     take(op_ref.at[:, pl.ds(0, SLAB // 2)], op_recv.at[1])
     adjoint_of(0, first, 1 - c)
-    forward = rest_of(0)
+    forward, _ = rest_of(0, lambda: None)
     second = stack(
         jnp.concatenate(whole[2:4], 0) - forward[0:2], jnp.concatenate(whole[6:8], 0) - forward[2:4]
     )
     adjoint_of(1, second, c)
     adjoint_of(1, second, 1 - c)
-    send_outs((forward, rest_of(1)))
+    forward_1, rows = rest_of(1, lambda: arrange(forward, jnp.zeros((32, 128), F32), 0))
+    send_outs(arrange(forward_1, rows, 4))
     back_0, back_1 = backs()
     residual = rest - back_0
     res_ref[...] = residual.reshape(2, 8, 256)
@@ -268,11 +306,18 @@
     take(op_ref.at[:, pl.ds(0, SLAB - 1)], op_send)
     take(spec_buf.at[pl.ds(0, NY * NZH - 1)], spec_send)
     take(co_buf.at[1, pl.ds(0, 3)], row_send)
-    take(co_buf.at[0], co_send.at[0])
-    take(co_buf.at[2], co_send.at[1])
+    def sent(buf, send):
+        @pl.when(below)
+        def _():
+            take(buf.at[0], send.at[0])
+
+        @pl.when(above)
+        def _():
+            take(buf.at[2], send.at[1])
+
+    sent(co_buf, co_send)
     for h in range(2):
-        take(halo.at[h, 0], halo_send.at[h, 0])
-        take(halo.at[h, 2], halo_send.at[h, 1])
+        sent(halo.at[h], halo_send.at[h])
         take(sums.at[h, pl.ds(0, NX - 1)], sum_send.at[h])
     take(out_buf.at[pl.ds(0, SLAB - 1)], out_send)
 

time: 93 us -> 87.2 us (0.938)
  Pallas kernels: 89.4 us -> 83.6 us
    pallas_call x1, Pallas kernels: 89.4 us -> 83.6 us  [body(): pl.pallas_call(kernel, out_shape=(jax.ShapeDtypeStruct(vectors.shape, F32...]
where the time goes in v4:
time: 87.2 us; the launch traced here: 86.9 us
  Pallas kernels  83.6 us (96%)
  local copies, waits for them, and re-layouts  2.65 us (3%)
    pallas_call x1, Pallas kernels, body(): pl.pallas_call(kernel, out_shape=(jax.ShapeDtypeStruct(vectors.shape, F32...  83.6 us
    unnamed x2, local copies, waits for them, and re-layouts  2.65 us

profile of v4, /device:TPU:1, one launch (start us, length us, event | category | flops | bytes accessed | tf_op | source)
XLA Modules:
  0.0 86.9 jit_solution(1089929454614767890)
XLA Ops:
  0.6 83.6 %shard_map.86 = (f32[2,8,256]{2,1,0:T(8,128)}, f32[2,8,256]{2,1,0:T(8,128)}) custom-call(f32[2,8,256]{2,1,0:T(8,128)} %vec_hbm.1, f32[2,8,256]{2,1,0:T(8,128)} %obs_hbm.1, bf16[2,128,8,384]{3,2,1,0:T(8,128)(2,1)} %op_ref.1, f32[1,8]{1,0:T(1,128)} %bitcast.1, f32[1,384]{1,0:T(1,128)} %coef_hbm.1, s32[1,384]{1,0:T(1,128)} %offs_hbm.1, ...), custom_call_target="tpu_custom_call" | custom-call | tf_op jit(solution)/shard_map/pallas_call | solution.py:328
  84.2 1.3 %copy.11 = f32[2,8,256]{2,1,0:T(8,128)} copy(f32[2,8,256]{2,1,0:T(8,128)} %get-tuple-element.4) | data formatting | bytes 32768
  85.6 1.3 %copy.12 = f32[2,8,256]{2,1,0:T(8,128)} copy(f32[2,8,256]{2,1,0:T(8,128)} %get-tuple-element.5) | data formatting | bytes 32768

commit v5 on v4

v5 whole, which is shorter than its diff:
```python
import math

import jax
import jax.numpy as jnp
import numpy as np
from jax import lax
from jax.experimental import pallas as pl
from jax.experimental.pallas import tpu as pltpu
from jax.sharding import PartitionSpec as P

SWEEPS = 4
NY, NZH, NX, NZL = 8, 4, 4, 2
NZ = NZH * NZL
F32, BF16 = jnp.float32, jnp.bfloat16


def basis_rows(length):
    half = length // 2
    freqs = np.arange(half)[:, None]
    times = np.arange(length)[None, :]
    angle = ((2 * freqs + 1) * times % (2 * length)) * (math.pi / length)
    scale = math.sqrt(2.0 / length)
    return np.concatenate([np.cos(angle) * scale, np.sin(angle) * scale], 1).astype(np.float32)


def basis_split(rows):
    rest = np.concatenate(np.split(rows, 2, axis=1), 0)
    pieces = []
    for _ in range(3):
        pieces.append(rest.astype(BF16))
        rest = rest - pieces[-1].astype(np.float32)
    return np.stack(pieces)


def dot_rows(a, b, **kw):
    return lax.dot_general(a, b, (((1,), (1,)), ((), ())), preferred_element_type=F32, **kw)


def kernel(
    vec_hbm, obs_hbm, op_ref, noise_hbm, coef_hbm, offs_hbm, basis_hbm, split_hbm,
    res_ref, app_ref,
    vec_ref, obs_ref, noise_ref, coef_ref, offs_ref, basis_ref, split_ref,
    a_buf, b_buf, w_buf, spec_own, spec_row, spec_buf, co_buf, halo, sums, out_own, out_row, out_buf,
    load_sem, op_local, one_send, one_recv, two_send, two_recv,
    spec_send, spec_recv, spec_send_2, spec_recv_2, row_send, row_recv, co_send, co_recv,
    halo_send, halo_recv, sum_send, sum_recv, out_send, out_recv, out_send_2, out_recv_2,
):
    sen = lax.axis_index("sen")
    par = lax.axis_index("par")
    x, q_me = lax.div(par, 4), lax.rem(par, 4)
    zl, c = lax.div(q_me, 2), lax.rem(q_me, 2)

    def wrap(value, size):
        return jnp.where(value >= size, value - size, value)

    def at(sen2, par2):
        return sen2 * (4 * NX) + par2

    def in_x(dx):
        return at(sen, wrap(x + dx, NX) * 4 + q_me)

    y, zh = lax.div(sen, NZH), lax.rem(sen, NZH)
    zc = zh * 4 + q_me
    far_y = (4, 3, 5, 2, 6, 1, 7)
    far_z = [(dz, dq) for dz in (2, 1, 3, 0) for dq in range(4) if dz or dq]

    def dev(y2, zh2, q2):
        return at(y2 * NZH + zh2, x * 4 + q2)

    def in_y(dy):
        return wrap(y + dy, NY)

    def in_z(dz, dq):
        return wrap(zh + dz, NZH), wrap(q_me + dq, 4)

    def remote(src, dst, send, recv, device):
        copy = pltpu.make_async_remote_copy(
            src_ref=src, dst_ref=dst, send_sem=send, recv_sem=recv,
            device_id=device, device_id_type=pl.DeviceIdType.LOGICAL,
        )
        copy.start()

    def take(ref, sem):
        pltpu.make_async_copy(ref, ref, sem).wait()

    barrier = pltpu.get_barrier_semaphore()

    def tell(device):
        pl.semaphore_signal(barrier, inc=1, device_id=device, device_id_type=pl.DeviceIdType.LOGICAL)

    for dy in far_y:
        tell(dev(in_y(dy), zh, q_me))
    for dz, dq in far_z:
        tell(dev(y, *in_z(dz, dq)))
    for dx in range(1, NX):
        tell(in_x(dx))

    loads = []
    for i, (src, dst) in enumerate(
        ((vec_hbm, vec_ref), (obs_hbm, obs_ref), (noise_hbm, noise_ref),
         (coef_hbm, coef_ref), (offs_hbm, offs_ref), (basis_hbm, basis_ref), (split_hbm, split_ref))
    ):
        loads.append(pltpu.make_async_copy(src, dst, load_sem.at[i]))
        loads[-1].start()

    own = [
        pltpu.make_async_copy(op_ref.at[0, y], a_buf.at[y], op_local.at[0]),
        pltpu.make_async_copy(op_ref.at[1, :, zc], b_buf.at[c, zl, zh], op_local.at[1]),
    ]
    for copy in own:
        copy.start()

    pl.semaphore_wait(barrier, 22 + NX - 1)

    half_y, half_z = lax.div(y, 4), lax.div(zh, 2)

    def first_stage(sub):
        to_y = 1 - half_y if sub == 0 else half_y
        to_z = 1 - half_z if sub == 0 else half_z
        cut_y = pl.ds(to_y * 4, 4)
        cut_z = pl.ds(to_z * 8, 8)
        for n, (dz, dq) in enumerate(far_z):
            if n % 2 == 0 and n // 2 < 7:
                y2 = in_y(far_y[n // 2])
                remote(
                    op_ref.at[0, y2, cut_z], a_buf.at[y, cut_z],
                    one_send.at[0], one_recv.at[0, sub], dev(y2, zh, q_me),
                )
            zh2, q2 = in_z(dz, dq)
            remote(
                op_ref.at[1, cut_y, zh2 * 4 + q2], b_buf.at[c, zl, zh, cut_y],
                one_send.at[1], one_recv.at[1, sub], dev(y, zh2, q2),
            )

    first_stage(0)

    for load in loads[:6]:
        load.wait()
    eye = lax.broadcasted_iota(jnp.int32, (8, 8), 0) == lax.broadcasted_iota(jnp.int32, (8, 8), 1)
    noise = jnp.sum(jnp.where(eye, noise_ref[...], 0.0), axis=1, keepdims=True)
    noise16 = jnp.concatenate([noise, noise], axis=0)
    vec = vec_ref[...].reshape(16, 256)
    rest = obs_ref[...].reshape(16, 256) - noise16 * vec
    record = jnp.concatenate([vec, rest], axis=0)
    blank = jnp.zeros_like(record)
    both = jnp.concatenate(
        [jnp.concatenate([record, blank], 1), jnp.concatenate([blank, record], 1), jnp.zeros((64, 512), F32)], 0
    )
    spec_own[...] = dot_rows(basis_ref[...], both, precision=lax.Precision.HIGHEST)

    co_buf[1, q_me, :, 0:384] = coef_ref[...]
    co_buf[1, q_me, :, 384:768] = offs_ref[...].astype(F32)

    for dy in far_y:
        y2 = in_y(dy)
        rows = pl.ds(pl.multiple_of(y2 * 16, 16), 16)
        remote(spec_own.at[rows], spec_row.at[y], spec_send, spec_recv, dev(y2, zh, q_me))
    for dq in range(1, 4):
        remote(co_buf.at[1, q_me], co_buf.at[1, q_me], row_send, row_recv, dev(y, zh, wrap(q_me + dq, 4)))

    first_stage(1)

    take(co_buf.at[1, pl.ds(0, 3)], row_recv)
    above, below = x > 0, x < NX - 1

    def to_neighbours(buf, send, recv):
        @pl.when(below)
        def _():
            remote(buf.at[1], buf.at[0], send.at[0], recv.at[0], par_at(x + 1))

        @pl.when(above)
        def _():
            remote(buf.at[1], buf.at[2], send.at[1], recv.at[1], par_at(x - 1))

    def from_neighbours(buf, recv):
        @pl.when(above)
        def _():
            take(buf.at[0], recv.at[0])

        @pl.when(below)
        def _():
            take(buf.at[2], recv.at[1])

    def par_at(x2):
        return at(sen, x2 * 4 + q_me)

    def clear(buf):
        @pl.when(x == 0)
        def _():
            buf[0] = jnp.zeros(buf.shape[1:], F32)

        @pl.when(x == NX - 1)
        def _():
            buf[2] = jnp.zeros(buf.shape[1:], F32)

    clear(co_buf)
    for h in range(2):
        clear(halo.at[h])
    to_neighbours(co_buf, co_send, co_recv)

    take(spec_row.at[pl.ds(0, NY - 1)], spec_recv)
    spec_row[y] = spec_own[pl.ds(pl.multiple_of(y * 16, 16), 16), :]
    for dz in range(1, NZH):
        zh2 = wrap(zh + dz, NZH)
        rows = pl.ds(pl.multiple_of(lax.div(zh2, 2) * 8, 8), 8)
        remote(spec_row.at[:, rows], spec_buf.at[:, zh], spec_send_2, spec_recv_2, dev(y, zh2, q_me))

    def send_z(zh2, q2):
        remote(
            a_buf.at[:, zh2 * 4 + q2], w_buf.at[c, zl, 0, :, zh], two_send.at[0], two_recv.at[0], dev(y, zh2, q2)
        )

    def send_y(y2):
        remote(b_buf.at[:, :, :, y2], w_buf.at[:, :, 1, y], two_send.at[1], two_recv.at[1], dev(y2, zh, q_me))

    half_a = op_ref.at[0, pl.ds(0, NY - 1), pl.ds(0, 8)]
    half_b = op_ref.at[0, pl.ds(0, 4), pl.ds(0, 15)]
    whole_a = op_ref.at[0, pl.ds(0, NY - 1)]
    whole_b = op_ref.at[0, :, pl.ds(0, 15)]
    for copy in own:
        copy.wait()
    take(half_a, one_recv.at[0, 0])
    for low in range(2):
        for q2 in range(4):
            send_z((1 - half_z) * 2 + low, q2)
    take(half_b, one_recv.at[1, 0])
    for low in range(4):
        send_y((1 - half_y) * 4 + low)
    take(half_a, one_recv.at[0, 1])
    for q2 in range(4):
        send_z(half_z * 4 + 1 - zh, q2)
    for dq in range(1, 4):
        send_z(zh, wrap(q_me + dq, 4))
    take(half_b, one_recv.at[1, 1])
    for dy in range(1, 4):
        send_y(half_y * 4 + wrap(y - half_y * 4 + dy, 4))
    kept = [
        pltpu.make_async_copy(a_buf.at[:, zc], w_buf.at[c, zl, 0, :, zh], op_local.at[0]),
        pltpu.make_async_copy(b_buf.at[:, :, :, y], w_buf.at[:, :, 1, y], op_local.at[1]),
    ]
    for copy in kept:
        copy.start()

    from_neighbours(co_buf, co_recv)

    def rows_of(first):
        parts = []
        for b in range(3):
            for r in range(4):
                parts.append(jnp.broadcast_to(co_buf[b, r, :, first : first + 384], (4, 384)))
        return jnp.concatenate(parts, axis=0)

    coef = rows_of(0)
    column = lax.broadcasted_iota(jnp.int32, (48, 384), 1)
    offs = rows_of(384).astype(jnp.int32)
    landed = column + offs
    offs = jnp.where((landed >= 0) & (landed < 384), offs, 99)

    def sweep(field, top, low, high):
        here = slice(low - top, high - top)
        u = field[here]
        rows = field.shape[0]
        upper = pltpu.roll(field, 4, 0)[here]
        lower = pltpu.roll(field, rows - 4, 0)[here]
        near_off, across = offs[low:high], column[low:high]
        linked = jnp.zeros_like(u)
        for shift in range(-3, 4):
            moved = lower if shift == 0 else pltpu.roll(lower, (-shift) % 384, 1)
            linked = jnp.where(near_off == shift, moved, linked)
        left = jnp.where(across == 0, 0.0, pltpu.roll(u, 1, 1))
        right = jnp.where(across == 383, 0.0, pltpu.roll(u, 383, 1))
        return u + coef[low:high] * (left + right + upper + linked - 4.0 * u)

    def smooth(field):
        field = sweep(field, 0, 0, 48)
        field = sweep(field, 0, 8, 40)
        field = sweep(field, 8, 8, 40)
        return sweep(field, 8, 16, 32)

    take(spec_buf.at[:, pl.ds(0, NZH - 1)], spec_recv_2)
    mine = pl.ds(pl.multiple_of(lax.div(zc, 8) * 8, 8), 8)
    spec_buf[:, zh] = spec_row[:, mine, :]
    pick = lax.broadcasted_iota(jnp.int32, (32, 8, 128), 1) == lax.rem(zc, 8)
    gathered = jnp.sum(jnp.where(pick, spec_buf[...].reshape(32, 8, 128), 0.0), axis=1)
    lane = lax.broadcasted_iota(jnp.int32, (32, 128), 1)
    sensor_row = lax.broadcasted_iota(jnp.int32, (32, 256), 0)
    sensor_lane = lax.broadcasted_iota(jnp.int32, (32, 256), 1) // 8
    whole = []
    for q in range(8):
        piece = jnp.where(lane // 8 == q, gathered, 0.0)
        for shift in (8, 16, 32, 64):
            piece = piece + pltpu.roll(piece, shift, 1)
        piece = jnp.concatenate([piece, piece], axis=1)
        whole.append(jnp.sum(jnp.where(sensor_row == sensor_lane, piece, 0.0), axis=0, keepdims=True))

    def stack(re, im):
        re, im = re.astype(BF16).astype(F32), im.astype(BF16).astype(F32)
        return jnp.concatenate(
            [jnp.concatenate([re, im], 1), jnp.concatenate([im, -re], 1)], 0
        ).astype(BF16)

    def weights(core, low):
        return w_buf[core, low].reshape(512, 384)

    def adjoint_of(h, spectra):
        for q in range(4):
            halo[h, 1, q] = jnp.dot(spectra, weights(q % 2, q // 2), preferred_element_type=F32)

    def rest_of(h, meanwhile):
        to_neighbours(halo.at[h], halo_send.at[h], halo_recv.at[h])
        done = meanwhile()
        from_neighbours(halo.at[h], halo_recv.at[h])
        parts = [halo[h, b, r] for b in range(3) for r in range(4)]
        smoothed = smooth(jnp.concatenate(parts, axis=0))
        total = jnp.zeros((4, 512), F32)
        for q in range(4):
            prior = smoothed[4 * q : 4 * q + 4].astype(BF16)
            total = total + dot_rows(prior, weights(q % 2, q // 2))
        sums[h, x] = jnp.concatenate(
            [total[0:2, :256] - total[2:4, 256:], total[2:4, :256] + total[0:2, 256:]], 0
        )
        for dx in range(1, NX):
            remote(sums.at[h, x], sums.at[h, x], sum_send.at[h], sum_recv.at[h], in_x(dx))
        take(sums.at[h, pl.ds(0, NX - 1)], sum_recv.at[h])
        forward = ((sums[h, 0] + sums[h, 1]) + sums[h, 2]) + sums[h, 3]
        return forward, done

    def arrange(forward, rows, first):
        for q in range(4):
            piece = jnp.where(sensor_row == sensor_lane, jnp.broadcast_to(forward[q : q + 1], (32, 256)), 0.0)
            piece = piece[:, :128] + piece[:, 128:]
            for shift in (8, 16, 32, 64):
                piece = piece + pltpu.roll(piece, shift, 1)
            rows = jnp.where(lane // 8 == (q // 2) * 4 + first + q % 2, piece, rows)
        return rows

    def send_outs(rows):
        out_own[...] = rows.reshape(NY, NZH, 1, 128)

        for dy in far_y:
            y2 = in_y(dy)
            remote(out_own.at[y2], out_row.at[y], out_send, out_recv, dev(y2, zh, q_me))
        out_row[y] = out_own[y]
        take(out_row.at[pl.ds(0, NY - 1)], out_recv)
        for dz, dq in far_z:
            zh2, q2 = in_z(dz, dq)
            remote(out_row.at[:, zh2], out_buf.at[:, zc], out_send_2, out_recv_2, dev(y, zh2, q2))
        out_buf[:, zc] = out_row[:, zh]

    def backs():
        take(out_buf.at[:, pl.ds(0, 15)], out_recv_2)
        loads[6].wait()
        got = out_buf[...].reshape(128, 128)
        left = jnp.concatenate([got[:, :32], got[:, 32:64]], 0).T
        pieces = []
        for _ in range(3):
            pieces.append(left.astype(BF16))
            left = left - pieces[-1].astype(F32)
        total = jnp.zeros((32, 256), F32)
        for a, b in ((2, 0), (0, 2), (1, 1), (1, 0), (0, 1), (0, 0)):
            total = total + jnp.dot(pieces[a], split_ref[b], preferred_element_type=F32)
        return total[:16], total[16:]

    first = stack(jnp.concatenate(whole[0:2], 0), jnp.concatenate(whole[4:6], 0))
    for copy in kept:
        copy.wait()
    take(whole_b, two_recv.at[0])
    take(whole_a, two_recv.at[1])
    adjoint_of(0, first)
    forward, _ = rest_of(0, lambda: None)
    second = stack(
        jnp.concatenate(whole[2:4], 0) - forward[0:2], jnp.concatenate(whole[6:8], 0) - forward[2:4]
    )
    adjoint_of(1, second)
    forward_1, rows = rest_of(1, lambda: arrange(forward, jnp.zeros((32, 128), F32), 0))
    send_outs(arrange(forward_1, rows, 2))
    back_0, back_1 = backs()
    residual = rest - back_0
    res_ref[...] = residual.reshape(2, 8, 256)
    app_ref[...] = (back_1 + noise16 * residual).reshape(2, 8, 256)

    take(whole_a, one_send.at[0])
    take(whole_b, one_send.at[1])
    take(whole_b, two_send.at[0])
    take(whole_a, two_send.at[1])
    take(spec_row.at[pl.ds(0, NY - 1)], spec_send)
    take(spec_buf.at[:, pl.ds(0, NZH - 1)], spec_send_2)
    take(co_buf.at[1, pl.ds(0, 3)], row_send)
    def sent(buf, send):
        @pl.when(below)
        def _():
            take(buf.at[0], send.at[0])

        @pl.when(above)
        def _():
            take(buf.at[2], send.at[1])

    sent(co_buf, co_send)
    for h in range(2):
        sent(halo.at[h], halo_send.at[h])
        take(sums.at[h, pl.ds(0, NX - 1)], sum_send.at[h])
    take(out_row.at[pl.ds(0, NY - 1)], out_send)
    take(out_buf.at[:, pl.ds(0, 15)], out_send_2)


def body(vectors, observed, operator, noise, coefficient, offsets):
    rows = basis_rows(vectors.shape[-1])
    vmem = pl.BlockSpec(memory_space=pltpu.VMEM)
    dma = pltpu.SemaphoreType.DMA
    return pl.pallas_call(
        kernel,
        out_shape=(jax.ShapeDtypeStruct(vectors.shape, F32),) * 2,
        in_specs=[pl.BlockSpec(memory_space=pl.ANY)] * 8,
        out_specs=(vmem, vmem),
        scratch_shapes=[
            pltpu.VMEM((2, 8, 256), F32),
            pltpu.VMEM((2, 8, 256), F32),
            pltpu.VMEM((1, 8), F32),
            pltpu.VMEM((1, 384), F32),
            pltpu.VMEM((1, 384), jnp.int32),
            pltpu.VMEM((128, 512), F32),
            pltpu.VMEM((3, 256, 256), BF16),
            pltpu.VMEM((NY, 16, 8, 384), BF16),
            pltpu.VMEM((2, 2, NZH, NY, 8, 384), BF16),
            pltpu.VMEM((2, 2, 2, NY, NZH, 8, 384), BF16),
            pltpu.VMEM((128, 128), F32),
            pltpu.VMEM((NY, 16, 128), F32),
            pltpu.VMEM((NY, NZH, 8, 128), F32),
            pltpu.VMEM((3, 4, 1, 768), F32),
            pltpu.VMEM((2, 3, 4, 4, 384), F32),
            pltpu.VMEM((2, 4, 4, 256), F32),
            pltpu.VMEM((NY, NZH, 1, 128), F32),
            pltpu.VMEM((NY, NZH, 1, 128), F32),
            pltpu.VMEM((NY, 16, 1, 128), F32),
            dma((7,)), dma((2,)), dma((2,)), dma((2, 2)), dma((2,)), dma((2,)),
            dma, dma, dma, dma, dma, dma, dma((2,)), dma((2,)),
            dma((2, 2)), dma((2, 2)), dma((2,)), dma((2,)), dma, dma, dma, dma,
        ],
        compiler_params=pltpu.CompilerParams(
            collective_id=0, has_side_effects=True, vmem_limit_bytes=60 * 1024 * 1024
        ),
    )(vectors, observed, operator.reshape(2, NY, 16, 8, 384), noise.reshape(1, 8), coefficient, offsets, jnp.asarray(rows), jnp.asarray(basis_split(rows)))


def solution(mesh):
    placed = (
        P(None, "sen", None),
        P(None, "sen", None),
        P(None, None, "sen", "par"),
        P("sen"),
        P("par", None),
        P("par", None),
    )
    return jax.shard_map(
        body,
        mesh=mesh,
        in_specs=placed,
        out_specs=(P(None, "sen", None), P(None, "sen", None)),
        check_vma=False,
    )
```

time: 87.2 us -> 85.2 us (0.977)
  Pallas kernels: 83.6 us -> 81.6 us
    pallas_call x1, Pallas kernels: 83.6 us -> 81.6 us  [body(): pl.pallas_call(kernel, out_shape=(jax.ShapeDtypeStruct(vectors.shape, F32...]
where the time goes in v5:
time: 85.2 us; the launch traced here: 84.9 us
  Pallas kernels  81.6 us (96%)
  local copies, waits for them, and re-layouts  2.65 us (3%)
    pallas_call x1, Pallas kernels, body(): pl.pallas_call(kernel, out_shape=(jax.ShapeDtypeStruct(vectors.shape, F32...  81.6 us
    unnamed x2, local copies, waits for them, and re-layouts  2.65 us

profile of v5, /device:TPU:1, one launch (start us, length us, event | category | flops | bytes accessed | tf_op | source)
XLA Modules:
  0.0 84.9 jit_solution(18331938382415945898)
XLA Ops:
  0.6 81.6 %shard_map.95 = (f32[2,8,256]{2,1,0:T(8,128)}, f32[2,8,256]{2,1,0:T(8,128)}) custom-call(f32[2,8,256]{2,1,0:T(8,128)} %vec_hbm.1, f32[2,8,256]{2,1,0:T(8,128)} %obs_hbm.1, bf16[2,8,16,8,384]{4,3,2,1,0:T(8,128)(2,1)} %bitcast.2, f32[1,8]{1,0:T(1,128)} %bitcast.3, f32[1,384]{1,0:T(1,128)} %coef_hbm.1, s32[1,384]{1,0:T(1,128)} %offs_hbm.1, ...), custom_call_target="tpu_custom_call" | custom-call | tf_op jit(solution)/shard_map/pallas_call | solution.py:410
  82.2 1.3 %copy.12 = f32[2,8,256]{2,1,0:T(8,128)} copy(f32[2,8,256]{2,1,0:T(8,128)} %get-tuple-element.4) | data formatting | bytes 32768
  83.5 1.3 %copy.13 = f32[2,8,256]{2,1,0:T(8,128)} copy(f32[2,8,256]{2,1,0:T(8,128)} %get-tuple-element.5) | data formatting | bytes 32768

commit v6 on v5

--- a/solution.py
+++ b/solution.py
@@ -40,10 +40,10 @@
     vec_hbm, obs_hbm, op_ref, noise_hbm, coef_hbm, offs_hbm, basis_hbm, split_hbm,
     res_ref, app_ref,
     vec_ref, obs_ref, noise_ref, coef_ref, offs_ref, basis_ref, split_ref,
-    a_buf, b_buf, w_buf, spec_own, spec_row, spec_buf, co_buf, halo, sums, out_own, out_row, out_buf,
+    a_buf, b_buf, w_buf, spec_own, spec_row, spec_buf, co_buf, halo, sums, out_own, out_buf,
     load_sem, op_local, one_send, one_recv, two_send, two_recv,
     spec_send, spec_recv, spec_send_2, spec_recv_2, row_send, row_recv, co_send, co_recv,
-    halo_send, halo_recv, sum_send, sum_recv, out_send, out_recv, out_send_2, out_recv_2,
+    halo_send, halo_recv, sum_send, sum_recv, out_send, out_recv,
 ):
     sen = lax.axis_index("sen")
     par = lax.axis_index("par")
@@ -337,18 +337,22 @@
     def send_outs(rows):
         out_own[...] = rows.reshape(NY, NZH, 1, 128)
 
-        for dy in far_y:
-            y2 = in_y(dy)
-            remote(out_own.at[y2], out_row.at[y], out_send, out_recv, dev(y2, zh, q_me))
-        out_row[y] = out_own[y]
-        take(out_row.at[pl.ds(0, NY - 1)], out_recv)
-        for dz, dq in far_z:
-            zh2, q2 = in_z(dz, dq)
-            remote(out_row.at[:, zh2], out_buf.at[:, zc], out_send_2, out_recv_2, dev(y, zh2, q2))
-        out_buf[:, zc] = out_row[:, zh]
+        mine = out_buf.at[y * 16 + zc]
+        for dz in (2, 1, 3, 0):
+            zh2 = wrap(zh + dz, NZH)
+
+            def send_block(k, y2):
+                for q2 in range(4):
+                    remote(out_own.at[y2, zh2], mine, out_send, out_recv, dev(y2, zh2, q2))
+                return wrap(y2 + 1, NY)
+
+            lax.fori_loop(0, NY if dz else NY - 1, send_block, in_y(4 if dz else 1))
+        for dq in range(1, 4):
+            remote(out_own.at[y, zh], mine, out_send, out_recv, dev(y, zh, wrap(q_me + dq, 4)))
+        out_buf[y * 16 + zc] = out_own[y, zh]
 
     def backs():
-        take(out_buf.at[:, pl.ds(0, 15)], out_recv_2)
+        take(out_buf.at[pl.ds(0, NY * 16 - 1)], out_recv)
         loads[6].wait()
         got = out_buf[...].reshape(128, 128)
         left = jnp.concatenate([got[:, :32], got[:, 32:64]], 0).T
@@ -399,8 +403,7 @@
     for h in range(2):
         sent(halo.at[h], halo_send.at[h])
         take(sums.at[h, pl.ds(0, NX - 1)], sum_send.at[h])
-    take(out_row.at[pl.ds(0, NY - 1)], out_send)
-    take(out_buf.at[:, pl.ds(0, 15)], out_send_2)
+    take(out_buf.at[pl.ds(0, NY * 16 - 1)], out_send)
 
 
 def body(vectors, observed, operator, noise, coefficient, offsets):
@@ -430,11 +433,10 @@
             pltpu.VMEM((2, 3, 4, 4, 384), F32),
             pltpu.VMEM((2, 4, 4, 256), F32),
             pltpu.VMEM((NY, NZH, 1, 128), F32),
-            pltpu.VMEM((NY, NZH, 1, 128), F32),
-            pltpu.VMEM((NY, 16, 1, 128), F32),
+            pltpu.VMEM((NY * 16, 1, 128), F32),
             dma((7,)), dma((2,)), dma((2,)), dma((2, 2)), dma((2,)), dma((2,)),
             dma, dma, dma, dma, dma, dma, dma((2,)), dma((2,)),
-            dma((2, 2)), dma((2, 2)), dma((2,)), dma((2,)), dma, dma, dma, dma,
+            dma((2, 2)), dma((2, 2)), dma((2,)), dma((2,)), dma, dma,
         ],
         compiler_params=pltpu.CompilerParams(
             collective_id=0, has_side_effects=True, vmem_limit_bytes=60 * 1024 * 1024

time: 85.2 us -> 82.9 us (0.973)
  Pallas kernels: 81.6 us -> 79.3 us
    pallas_call x1, Pallas kernels: 81.6 us -> 79.3 us  [body(): pl.pallas_call(kernel, out_shape=(jax.ShapeDtypeStruct(vectors.shape, F32...]
where the time goes in v6:
time: 82.9 us; the launch traced here: 82.6 us
  Pallas kernels  79.3 us (96%)
  local copies, waits for them, and re-layouts  2.65 us (3%)
    pallas_call x1, Pallas kernels, body(): pl.pallas_call(kernel, out_shape=(jax.ShapeDtypeStruct(vectors.shape, F32...  79.3 us
    unnamed x2, local copies, waits for them, and re-layouts  2.65 us

profile of v6, /device:TPU:1, one launch (start us, length us, event | category | flops | bytes accessed | tf_op | source)
XLA Modules:
  0.0 82.6 jit_solution(16431313023120935810)
XLA Ops:
  0.6 79.3 %shard_map.95 = (f32[2,8,256]{2,1,0:T(8,128)}, f32[2,8,256]{2,1,0:T(8,128)}) custom-call(f32[2,8,256]{2,1,0:T(8,128)} %vec_hbm.1, f32[2,8,256]{2,1,0:T(8,128)} %obs_hbm.1, bf16[2,8,16,8,384]{4,3,2,1,0:T(8,128)(2,1)} %bitcast.2, f32[1,8]{1,0:T(1,128)} %bitcast.3, f32[1,384]{1,0:T(1,128)} %coef_hbm.1, s32[1,384]{1,0:T(1,128)} %offs_hbm.1, ...), custom_call_target="tpu_custom_call" | custom-call | tf_op jit(solution)/shard_map/pallas_call | solution.py:413
  79.9 1.3 %copy.12 = f32[2,8,256]{2,1,0:T(8,128)} copy(f32[2,8,256]{2,1,0:T(8,128)} %get-tuple-element.4) | data formatting | bytes 32768
  81.3 1.3 %copy.13 = f32[2,8,256]{2,1,0:T(8,128)} copy(f32[2,8,256]{2,1,0:T(8,128)} %get-tuple-element.5) | data formatting | bytes 32768

commit v7 on v6

--- a/solution.py
+++ b/solution.py
@@ -38,7 +38,7 @@
 
 def kernel(
     vec_hbm, obs_hbm, op_ref, noise_hbm, coef_hbm, offs_hbm, basis_hbm, split_hbm,
-    res_ref, app_ref,
+    out_ref,
     vec_ref, obs_ref, noise_ref, coef_ref, offs_ref, basis_ref, split_ref,
     a_buf, b_buf, w_buf, spec_own, spec_row, spec_buf, co_buf, halo, sums, out_own, out_buf,
     load_sem, op_local, one_send, one_recv, two_send, two_recv,
@@ -346,7 +346,9 @@
                     remote(out_own.at[y2, zh2], mine, out_send, out_recv, dev(y2, zh2, q2))
                 return wrap(y2 + 1, NY)
 
-            lax.fori_loop(0, NY if dz else NY - 1, send_block, in_y(4 if dz else 1))
+            y2 = in_y(4 if dz else 1)
+            for k in range(NY if dz else NY - 1):
+                y2 = send_block(k, y2)
         for dq in range(1, 4):
             remote(out_own.at[y, zh], mine, out_send, out_recv, dev(y, zh, wrap(q_me + dq, 4)))
         out_buf[y * 16 + zc] = out_own[y, zh]
@@ -380,8 +382,8 @@
     send_outs(arrange(forward_1, rows, 2))
     back_0, back_1 = backs()
     residual = rest - back_0
-    res_ref[...] = residual.reshape(2, 8, 256)
-    app_ref[...] = (back_1 + noise16 * residual).reshape(2, 8, 256)
+    out_ref[0] = residual.reshape(2, 8, 256)
+    out_ref[1] = (back_1 + noise16 * residual).reshape(2, 8, 256)
 
     take(whole_a, one_send.at[0])
     take(whole_b, one_send.at[1])
@@ -410,11 +412,11 @@
     rows = basis_rows(vectors.shape[-1])
     vmem = pl.BlockSpec(memory_space=pltpu.VMEM)
     dma = pltpu.SemaphoreType.DMA
-    return pl.pallas_call(
+    both = pl.pallas_call(
         kernel,
-        out_shape=(jax.ShapeDtypeStruct(vectors.shape, F32),) * 2,
+        out_shape=jax.ShapeDtypeStruct((2, *vectors.shape), F32),
         in_specs=[pl.BlockSpec(memory_space=pl.ANY)] * 8,
-        out_specs=(vmem, vmem),
+        out_specs=vmem,
         scratch_shapes=[
             pltpu.VMEM((2, 8, 256), F32),
             pltpu.VMEM((2, 8, 256), F32),
@@ -442,6 +444,7 @@
             collective_id=0, has_side_effects=True, vmem_limit_bytes=60 * 1024 * 1024
         ),
     )(vectors, observed, operator.reshape(2, NY, 16, 8, 384), noise.reshape(1, 8), coefficient, offsets, jnp.asarray(rows), jnp.asarray(basis_split(rows)))
+    return both[0], both[1]
 
 
 def solution(mesh):

time: 82.9 us -> 81.4 us (0.982)
  local copies, waits for them, and re-layouts: 2.65 us -> 1.35 us
    unnamed x2 -> x0, local copies, waits for them, and re-layouts: 2.65 us -> none
    squeeze x0 -> x1, local copies, waits for them, and re-layouts: none -> 1.35 us  [body(): return (both[0], both[1])]
where the time goes in v7:
time: 81.4 us; the launch traced here: 81.2 us
  Pallas kernels  79.2 us (97%)
  local copies, waits for them, and re-layouts  1.35 us (2%)
    pallas_call x1, Pallas kernels, body(): pl.pallas_call(kernel, out_shape=jax.ShapeDtypeStruct((2, *vectors.shape)...  79.2 us

profile of v7, /device:TPU:1, one launch (start us, length us, event | category | flops | bytes accessed | tf_op | source)
XLA Modules:
  0.0 81.2 jit_solution(159876667083700189)
XLA Ops:
  0.6 79.2 %shard_map.95 = f32[2,2,8,256]{3,2,1,0:T(8,128)} custom-call(f32[2,8,256]{2,1,0:T(8,128)} %vec_hbm.1, f32[2,8,256]{2,1,0:T(8,128)} %obs_hbm.1, bf16[2,8,16,8,384]{4,3,2,1,0:T(8,128)(2,1)} %bitcast.6, f32[1,8]{1,0:T(1,128)} %bitcast.7, f32[1,384]{1,0:T(1,128)} %coef_hbm.1, s32[1,384]{1,0:T(1,128)} %offs_hbm.1, f32[128,512]{1,0:T(8,128)} %constant.4.clone.basis_hbm, ...), custom_call_target="tpu_custom_call" | custom-call | tf_op jit(solution)/shard_map/pallas_call | solution.py:415
  79.9 1.3 %slice_bitcast_fusion = (f32[2,8,256]{2,1,0:T(8,128)}, f32[2,8,256]{2,1,0:T(8,128)}) fusion(f32[2,2,8,256]{3,2,1,0:T(8,128)} %shard_map.95), kind=kLoop, calls=%fused_computation | loop fusion | bytes 65536 | tf_op jit(solution)/shard_map/squeeze | solution.py:447
